TPU v7x, 32 devices: a whole 2x2x4 slice. The times are simulated.
32 devices in a mesh: dp: 8 (over y, x, core), tensor: 4 (over z).
Axes of the slice: x: 2, y: 2, z: 4, core: 2. Of those that a mesh axis runs over, the one named last changes fastest.
Arguments:
- frames: bfloat16 [8192, 1024], P('dp'), may hold values from -6 to 6
- skip_in: bfloat16 [8192, 1024], P('dp'), may hold values from -6 to 6
- flow_time: float32 [8], P('dp'), may hold values from 0 to 1
- segment_ids: int32 [8, 1024], P('dp'), may hold values from 0 to 3, never falling along the last dimension, each value on 1 to 512 neighbouring positions
- w_skip: bfloat16 [2048, 1024], P(None, 'tensor'), may hold values from -0.125 to 0.125
- b_skip: float32 [1024], P('tensor'), may hold values from -1.5 to 1.5
- w_modulation: bfloat16 [1024, 6144], P(None, 'tensor'), may hold values from -0.1875 to 0.1875
- b_modulation: float32 [6144], P('tensor'), may hold values from -4 to 4
- w_query: bfloat16 [1024, 1024], P(None, 'tensor'), may hold values from -0.1875 to 0.1875
- w_key: bfloat16 [1024, 1024], P(None, 'tensor'), may hold values from -0.1875 to 0.1875
- w_value: bfloat16 [1024, 1024], P(None, 'tensor'), may hold values from -0.1875 to 0.1875
- w_out: bfloat16 [1024, 1024], P('tensor'), may hold values from -0.75 to 0.75
- w_up: bfloat16 [1024, 4096], P(None, 'tensor'), may hold values from -0.1875 to 0.1875
- b_up: float32 [4096], P('tensor'), may hold values from -2.5 to 2.5
- w_down: bfloat16 [4096, 1024], P('tensor'), may hold values from -0.09375 to 0.09375
- b_down: float32 [1024], replicated, may hold values from -2.5 to 2.5
- out_grad: bfloat16 [8192, 1024], P('dp'), may hold values from -6 to 6
Outputs:
- output: float32 [8192, 1024], P('dp', 'tensor')
- grad_frames: float32 [8192, 1024], P('dp', 'tensor')
- grad_skip: float32 [8192, 1024], P('dp', 'tensor')
- grad_w_skip: float32 [2048, 1024], P('dp', 'tensor')
- grad_b_skip: float32 [1024], P(('tensor', 'dp'))
- grad_w_modulation: float32 [1024, 6144], P('dp', 'tensor')
- grad_b_modulation: float32 [6144], P(('tensor', 'dp'))
- grad_w_query: float32 [1024, 1024], P('dp', 'tensor')
- grad_w_key: float32 [1024, 1024], P('dp', 'tensor')
- grad_w_value: float32 [1024, 1024], P('dp', 'tensor')
- grad_w_out: float32 [1024, 1024], P('tensor', 'dp')
- grad_w_up: float32 [1024, 4096], P('dp', 'tensor')
- grad_b_up: float32 [4096], P(('tensor', 'dp'))
- grad_w_down: float32 [4096, 1024], P('tensor', 'dp')
- grad_b_down: float32 [1024], P('dp')
Inputs may be any that keep to these rules, and one draw needn't show every extreme that they name: `segment_ids`: within each packed row of 1024 frames the ids run 0 to 3 in order and never fall; each utterance has 1 to 512 frames, one exactly that many.
All inputs are finite; a program needn't handle non-finite values.
Results may differ from a plain program's by a relative error of at most 0.018.
Values sent between devices are 32-bit elements; how exact they have to be, the bound alone decides.
A program may use at most 192 MiB of HBM per device.

v0:
```python
import math

import jax
import jax.numpy as jnp
from jax import lax
from jax.sharding import PartitionSpec as P

HEAD_DIM = 64


EPS = 1e-06


def normalize(values):
    mean_val = jnp.mean(values, axis=-1, keepdims=True)
    centred = values - mean_val
    var_val = jnp.mean(centred * centred, axis=-1, keepdims=True)
    return centred * lax.rsqrt(var_val + EPS)


def modulate(hidden, shift, scale):
    return normalize(hidden) * (1.0 + scale[:, None, :]) + shift[:, None, :]


def time_embed(flow_time, width):
    half = width // 2
    freqs = jnp.exp(-math.log(10000.0) * jnp.arange(half, dtype=jnp.float32) / half)
    angles = 1000.0 * flow_time[:, None] * freqs[None, :]
    return jnp.concatenate([jnp.cos(angles), jnp.sin(angles)], axis=1)


def rotary_tables(segment_ids, head_dim):
    length = segment_ids.shape[1]
    steps = jnp.arange(length, dtype=jnp.int32)[None, :]
    starts_here = jnp.concatenate(
        [jnp.ones_like(segment_ids[:, :1], dtype=bool), segment_ids[:, 1:] != segment_ids[:, :-1]],
        axis=1,
    )
    first = lax.cummax(jnp.where(starts_here, steps, 0), axis=1)
    places = (steps - first).astype(jnp.float32)
    half = head_dim // 2
    inverse = jnp.exp(-math.log(10000.0) * 2.0 * jnp.arange(half, dtype=jnp.float32) / head_dim)
    angles = places[:, :, None] * inverse[None, None, :]
    return (jnp.cos(angles), jnp.sin(angles))


def rotate(values, cos_t, sin_t):
    half = values.shape[-1] // 2
    first = values[..., :half]
    second = values[..., half:]
    cos_e = cos_t[:, :, None, :]
    sin_e = sin_t[:, :, None, :]
    return jnp.concatenate(
        [first * cos_e - second * sin_e, second * cos_e + first * sin_e], axis=-1
    )


def gelu_tanh(values):
    return jax.nn.gelu(values, approximate=True)


def attention_forward(query, key, value, segment_ids, block):
    rows, length, heads, head_dim = query.shape
    count = length // block
    scale = head_dim ** (-0.5)

    def one_block(index):
        row = index // count
        start = index % count * block
        q_row = lax.dynamic_index_in_dim(query, row, 0, keepdims=False)
        k_row = lax.dynamic_index_in_dim(key, row, 0, keepdims=False)
        v_row = lax.dynamic_index_in_dim(value, row, 0, keepdims=False)
        seg_row = lax.dynamic_index_in_dim(segment_ids, row, 0, keepdims=False)
        q_blk = lax.dynamic_slice_in_dim(q_row, start, block, 0)
        seg_blk = lax.dynamic_slice_in_dim(seg_row, start, block, 0)
        scores = (
            jnp.einsum("qhd,khd->hqk", q_blk, k_row, preferred_element_type=jnp.float32) * scale
        )
        same = seg_blk[:, None] == seg_row[None, :]
        scores = jnp.where(same[None], scores, -1e30)
        top = jnp.max(scores, axis=-1, keepdims=True)
        expo = jnp.exp(scores - top)
        total = jnp.sum(expo, axis=-1, keepdims=True)
        probs = (expo / total).astype(jnp.bfloat16)
        result = jnp.einsum("hqk,khd->qhd", probs, v_row, preferred_element_type=jnp.float32)
        return (result.astype(jnp.bfloat16), (top + jnp.log(total))[..., 0])

    results, lse = lax.map(one_block, jnp.arange(rows * count, dtype=jnp.int32))
    return (results.reshape(rows, length, heads, head_dim), lse)


def attention_backward(query, key, value, segment_ids, lse, grad_att, block):
    rows, length, heads, head_dim = query.shape
    count = length // block
    scale = head_dim ** (-0.5)

    def attention_per_row(row):
        q_row = lax.dynamic_index_in_dim(query, row, 0, keepdims=False)
        k_row = lax.dynamic_index_in_dim(key, row, 0, keepdims=False)
        v_row = lax.dynamic_index_in_dim(value, row, 0, keepdims=False)
        seg_row = lax.dynamic_index_in_dim(segment_ids, row, 0, keepdims=False)
        g_row = lax.dynamic_index_in_dim(grad_att, row, 0, keepdims=False)

        def step(carry, blk):
            key_acc, value_acc = carry
            start = blk * block
            q_blk = lax.dynamic_slice_in_dim(q_row, start, block, 0)
            g_blk = lax.dynamic_slice_in_dim(g_row, start, block, 0)
            seg_blk = lax.dynamic_slice_in_dim(seg_row, start, block, 0)
            lse_blk = lax.dynamic_index_in_dim(lse, row * count + blk, 0, keepdims=False)
            scores = (
                jnp.einsum("qhd,khd->hqk", q_blk, k_row, preferred_element_type=jnp.float32) * scale
            )
            same = seg_blk[:, None] == seg_row[None, :]
            scores = jnp.where(same[None], scores, -1e30)
            probs = jnp.exp(scores - lse_blk[:, :, None])
            grad_p = jnp.einsum("qhd,khd->hqk", g_blk, v_row, preferred_element_type=jnp.float32)
            delta = jnp.sum(probs * grad_p, axis=-1, keepdims=True)
            grad_s = (probs * (grad_p - delta)).astype(jnp.bfloat16)
            q_grad = (
                jnp.einsum("hqk,khd->qhd", grad_s, k_row, preferred_element_type=jnp.float32)
                * scale
            )
            key_acc = (
                key_acc
                + jnp.einsum("hqk,qhd->khd", grad_s, q_blk, preferred_element_type=jnp.float32)
                * scale
            )
            value_acc = value_acc + jnp.einsum(
                "hqk,qhd->khd",
                probs.astype(jnp.bfloat16),
                g_blk,
                preferred_element_type=jnp.float32,
            )
            return ((key_acc, value_acc), q_grad)

        zeros = jnp.zeros((length, heads, head_dim), jnp.float32)
        (k_grad, v_grad), q_grads = lax.scan(
            step, (zeros, zeros), jnp.arange(count, dtype=jnp.int32)
        )
        return (q_grads.reshape(length, heads, head_dim), k_grad, v_grad)

    return lax.map(attention_per_row, jnp.arange(rows, dtype=jnp.int32))


def per_device(
    frames,
    skip_in,
    flow_time,
    segment_ids,
    w_skip,
    b_skip,
    w_modulation,
    b_modulation,
    w_query,
    w_key,
    w_value,
    w_out,
    w_up,
    b_up,
    w_down,
    b_down,
    out_grad,
):
    rows, length = segment_ids.shape
    tokens, width = frames.shape
    local = w_query.shape[1]
    heads = local // HEAD_DIM
    block = min(512, length)
    tensor_pos = lax.axis_index("tensor")

    def body_per_row(values, vector):
        return (values.reshape(rows, length, -1) * vector[:, None, :]).reshape(tokens, -1)

    def row_sums(values):
        return jnp.sum(values.reshape(rows, length, -1), axis=1)

    def own_cols(values):
        return lax.dynamic_slice_in_dim(values, tensor_pos * local, local, values.ndim - 1)

    joined = jnp.concatenate([frames, skip_in], axis=1)
    skip_part = jnp.dot(joined, w_skip, preferred_element_type=jnp.float32) + b_skip
    embed = jax.nn.silu(time_embed(flow_time, width)).astype(jnp.bfloat16)
    mod_part = jnp.dot(embed, w_modulation, preferred_element_type=jnp.float32) + b_modulation
    hidden, mod = (
        lax.all_gather(skip_part, "tensor", axis=1, tiled=True),
        lax.all_gather(mod_part, "tensor", axis=1, tiled=True),
    )
    shift1, scale1, gate1, shift2, scale2, gate2 = [
        mod[:, i * width : (i + 1) * width] for i in range(6)
    ]
    hidden3 = hidden.reshape(rows, length, width)
    normed = modulate(hidden3, shift1, scale1).reshape(tokens, width).astype(jnp.bfloat16)
    cos_t, sin_t = rotary_tables(segment_ids, HEAD_DIM)

    def heads_of(weight):
        return jnp.dot(normed, weight, preferred_element_type=jnp.float32).reshape(
            rows, length, heads, HEAD_DIM
        )

    query = rotate(heads_of(w_query), cos_t, sin_t).astype(jnp.bfloat16)
    key = rotate(heads_of(w_key), cos_t, sin_t).astype(jnp.bfloat16)
    value = heads_of(w_value).astype(jnp.bfloat16)
    attended, lse = attention_forward(query, key, value, segment_ids, block)
    attended_flat = attended.reshape(tokens, local)
    branch = lax.psum(jnp.dot(attended_flat, w_out, preferred_element_type=jnp.float32), "tensor")
    mid = hidden + body_per_row(branch, gate1)
    mid3 = mid.reshape(rows, length, width)
    normed2 = modulate(mid3, shift2, scale2).reshape(tokens, width).astype(jnp.bfloat16)
    pre = jnp.dot(normed2, w_up, preferred_element_type=jnp.float32) + b_up
    act = gelu_tanh(pre).astype(jnp.bfloat16)
    ffn_term = jnp.dot(act, w_down, preferred_element_type=jnp.float32)
    grad_out = out_grad.astype(jnp.float32)
    ffn = lax.psum(ffn_term, "tensor") + b_down
    output = mid + body_per_row(ffn, gate2)
    own_output = own_cols(output)
    grad_gate2 = row_sums(grad_out * ffn)
    grad_ffn = body_per_row(grad_out, gate2)
    grad_b_down = jnp.sum(grad_ffn, axis=0)
    grad_ffn_low = grad_ffn.astype(jnp.bfloat16)
    grad_act = jnp.einsum("td,fd->tf", grad_ffn_low, w_down, preferred_element_type=jnp.float32)
    gelu_pull = jax.vjp(gelu_tanh, pre)[1]
    grad_pre = gelu_pull(grad_act)[0].astype(jnp.bfloat16)
    grad_w_down = jnp.einsum("tf,td->fd", act, grad_ffn_low, preferred_element_type=jnp.float32)
    grad_w_up = jnp.einsum("td,tf->df", normed2, grad_pre, preferred_element_type=jnp.float32)
    grad_b_up = jnp.sum(grad_pre.astype(jnp.float32), axis=0)
    grad_normed2 = lax.psum(
        jnp.einsum("tf,df->td", grad_pre, w_up, preferred_element_type=jnp.float32), "tensor"
    )
    norm2_pull = jax.vjp(modulate, mid3, shift2, scale2)[1]
    grad_mid_add, grad_shift2, grad_scale2 = norm2_pull(grad_normed2.reshape(rows, length, width))
    grad_mid = grad_out + grad_mid_add.reshape(tokens, width)
    grad_gate1 = row_sums(grad_mid * branch)
    grad_branch = body_per_row(grad_mid, gate1).astype(jnp.bfloat16)
    grad_w_out = jnp.einsum(
        "te,td->ed", attended_flat, grad_branch, preferred_element_type=jnp.float32
    )
    grad_att = jnp.einsum(
        "td,ed->te", grad_branch, w_out, preferred_element_type=jnp.float32
    ).astype(jnp.bfloat16)
    grad_att = grad_att.reshape(rows, length, heads, HEAD_DIM)
    grad_q_rot, grad_k_rot, grad_v = attention_backward(
        query, key, value, segment_ids, lse, grad_att, block
    )
    grad_query = rotate(grad_q_rot, cos_t, -sin_t).reshape(tokens, local).astype(jnp.bfloat16)
    grad_key = rotate(grad_k_rot, cos_t, -sin_t).reshape(tokens, local).astype(jnp.bfloat16)
    grad_value = grad_v.reshape(tokens, local).astype(jnp.bfloat16)
    grad_w_query = jnp.einsum("td,te->de", normed, grad_query, preferred_element_type=jnp.float32)
    grad_w_key = jnp.einsum("td,te->de", normed, grad_key, preferred_element_type=jnp.float32)
    grad_w_value = jnp.einsum("td,te->de", normed, grad_value, preferred_element_type=jnp.float32)
    normed_part = jnp.einsum("te,de->td", grad_query, w_query, preferred_element_type=jnp.float32)
    normed_part = normed_part + jnp.einsum(
        "te,de->td", grad_key, w_key, preferred_element_type=jnp.float32
    )
    normed_part = normed_part + jnp.einsum(
        "te,de->td", grad_value, w_value, preferred_element_type=jnp.float32
    )
    grad_normed = lax.psum(normed_part, "tensor")
    norm1_pull = jax.vjp(modulate, hidden3, shift1, scale1)[1]
    grad_hid_add, grad_shift1, grad_scale1 = norm1_pull(grad_normed.reshape(rows, length, width))
    grad_hidden = grad_mid + grad_hid_add.reshape(tokens, width)
    own_grad = own_cols(grad_hidden)
    grad_b_skip = jnp.sum(own_grad, axis=0)
    own_low = own_grad.astype(jnp.bfloat16)
    grad_w_skip = jnp.einsum("tc,td->cd", joined, own_low, preferred_element_type=jnp.float32)
    grad_joined = jnp.einsum("td,cd->tc", own_low, w_skip, preferred_element_type=jnp.float32)
    grad_frames, grad_skip = (
        lax.psum_scatter(grad_joined[:, :width], "tensor", scatter_dimension=1, tiled=True),
        lax.psum_scatter(grad_joined[:, width:], "tensor", scatter_dimension=1, tiled=True),
    )
    grad_mod = jnp.concatenate(
        [grad_shift1, grad_scale1, grad_gate1, grad_shift2, grad_scale2, grad_gate2], axis=1
    )
    own_mod = lax.dynamic_slice_in_dim(grad_mod, tensor_pos * 6 * local, 6 * local, 1)
    grad_b_mod = jnp.sum(own_mod, axis=0)
    grad_w_mod = jnp.einsum(
        "rd,re->de", embed, own_mod.astype(jnp.bfloat16), preferred_element_type=jnp.float32
    )
    (
        s_w_skip,
        s_b_skip,
        s_w_mod,
        s_b_mod,
        s_w_query,
        s_w_key,
        s_w_value,
        s_w_out,
        s_w_up,
        s_b_up,
        s_w_down,
        s_b_down,
    ) = (
        lax.psum_scatter(grad_w_skip, "dp", scatter_dimension=0, tiled=True),
        lax.psum_scatter(grad_b_skip, "dp", scatter_dimension=0, tiled=True),
        lax.psum_scatter(grad_w_mod, "dp", scatter_dimension=0, tiled=True),
        lax.psum_scatter(grad_b_mod, "dp", scatter_dimension=0, tiled=True),
        lax.psum_scatter(grad_w_query, "dp", scatter_dimension=0, tiled=True),
        lax.psum_scatter(grad_w_key, "dp", scatter_dimension=0, tiled=True),
        lax.psum_scatter(grad_w_value, "dp", scatter_dimension=0, tiled=True),
        lax.psum_scatter(grad_w_out, "dp", scatter_dimension=1, tiled=True),
        lax.psum_scatter(grad_w_up, "dp", scatter_dimension=0, tiled=True),
        lax.psum_scatter(grad_b_up, "dp", scatter_dimension=0, tiled=True),
        lax.psum_scatter(grad_w_down, "dp", scatter_dimension=1, tiled=True),
        lax.psum_scatter(grad_b_down, "dp", scatter_dimension=0, tiled=True),
    )
    return (
        own_output,
        grad_frames,
        grad_skip,
        s_w_skip,
        s_b_skip,
        s_w_mod,
        s_b_mod,
        s_w_query,
        s_w_key,
        s_w_value,
        s_w_out,
        s_w_up,
        s_b_up,
        s_w_down,
        s_b_down,
    )


def solution(mesh):
    in_specs = (
        P("dp", None),
        P("dp", None),
        P("dp"),
        P("dp", None),
        P(None, "tensor"),
        P("tensor"),
        P(None, "tensor"),
        P("tensor"),
        P(None, "tensor"),
        P(None, "tensor"),
        P(None, "tensor"),
        P("tensor", None),
        P(None, "tensor"),
        P("tensor"),
        P("tensor", None),
        P(),
        P("dp", None),
    )
    out_specs = (
        P("dp", "tensor"),
        P("dp", "tensor"),
        P("dp", "tensor"),
        P("dp", "tensor"),
        P(("tensor", "dp")),
        P("dp", "tensor"),
        P(("tensor", "dp")),
        P("dp", "tensor"),
        P("dp", "tensor"),
        P("dp", "tensor"),
        P("tensor", "dp"),
        P("dp", "tensor"),
        P(("tensor", "dp")),
        P("tensor", "dp"),
        P("dp"),
    )
    return jax.shard_map(
        per_device, mesh=mesh, in_specs=in_specs, out_specs=out_specs, check_vma=False
    )
```

profile of v0, /device:TPU:0, one launch (start us, length us, event | category | flops | bytes accessed | tf_op | source)
XLA Modules:
  0.0 1384.0 jit_solution(6972249847221236484)
XLA Ops:
  7.3 1.9 constant_dynamic-update-slice_fusion.1
  9.9 2.0 copy-done.30
  11.9 2.2 convolution_add_fusion
  19.4 2.0 copy.43
  21.5 16.4 %all-gather.1 = f32[4,1,1536]{2,1,0:T(1,128)S(1)} all-gather(f32[1,1,1536]{2,1,0:T(1,128)S(1)} %reshape.732), channel_id=2, replica_groups=mesh['dp'=8,'tensor'=4] {'tensor'}, dimensions={0}, use_global_device_ids=true | all-gather | bytes 30720 | tf_op jit(solution)/shard_map/all_gather | solution.py:187
  39.2 58.8 %all-gather.4.cloned.1.call-done = f32[1024,1024]{1,0:T(8,128)} async-done(((f32[1024,256]{1,0:T(8,128)}), f32[1024,1024]{1,0:T(8,128)}) %all-gather.4.cloned.1.call-update) | async-done | bytes 4194320 | tf_op jit(solution)/shard_map/all_gather | solution.py:186
  98.0 2.4 reduce_sum.191
  100.5 2.9 multiply_reduce_fusion.7
  108.2 22.9 %while.43 = (s32[]{:T(128)}, bf16[2,512,4,64]{1,3,2,0:T(8,128)(2,1)}, f32[2,4,512]{2,1,0:T(4,128)S(1)}, s32[2]{0:T(128)S(1)}, s32[1,1024]{1,0:T(1,128)S(1)}, /*i...) while((s32[]{:T(128)}, ...), condition=%wide.region_7.8_spmd, body=%wide.region_4.7_spmd.sunk | while | flops 562690048 | bytes 33106292 | solution.py:88
  111.2 1.7 fusion.154
  112.9 2.3 fusion.155
  115.2 3.7 fusion.156
  122.6 1.7 fusion.154
  124.3 2.3 fusion.155
  126.7 3.7 fusion.156
  131.1 1.6 copy.44
  132.8 2.7 fusion.91
  135.7 153.4 %all-reduce.10.cloned.1.call-done = f32[1024,1024]{1,0:T(8,128)} async-done(((f32[1024,1024]{1,0:T(8,128)}), f32[1024,1024]{1,0:T(8,128)}) %all-reduce.10.cloned.1.call-update) | async-done | bytes 4194320 | tf_op jit(solution)/shard_map/psum | solution.py:206
  289.2 4.0 fusion.89
  293.8 2.5 copy-done.55
  296.3 2.5 fusion.84
  298.8 5.7 convert_reduce_fusion
  305.9 4.3 fusion.92
  310.4 7.6 fusion.82
  318.0 146.4 %all-reduce.12.cloned.1.call-done = f32[1024,1024]{1,0:T(8,128)} async-done(((f32[1024,1024]{1,0:T(8,128)}), f32[1024,1024]{1,0:T(8,128)}) %all-reduce.12.cloned.1.call-update) | async-done | bytes 4194320 | tf_op jit(solution)/shard_map/psum | solution.py:227
  464.3 5.2 multiply_reduce_fusion.1
  470.3 1.7 fusion.88
  474.5 2.1 copy-done.8
  478.1 59.7 %while.44 = (s32[]{:T(128)}, f32[1024,4,64]{0,2,1:T(8,128)S(1)}, f32[1024,4,64]{0,2,1:T(8,128)}, f32[2,512,4,64]{1,0,3,2:T(2,128)}, s32[2]{0:T(128)S(1)}, /*inde...) while((s32[]{:T(128)}, f32[1024,4,64]{0,2,1:T(8,128)S(1)}, ...), condition=%wide.region_17.18_spmd.clone, body=%wide.region_15.17_spmd.clone.sunk | while | flops 1375598592 | bytes 74516760 | solution.py:138
  483.2 4.4 fusion.168
  487.7 4.3 multiply_reduce_fusion.9
  492.0 2.4 multiply_convert_fusion.10
  497.3 10.4 dynamic_update_slice.37
  512.6 4.8 fusion.168
  517.4 4.3 multiply_reduce_fusion.9
  521.7 2.4 multiply_convert_fusion.10
  527.0 10.4 dynamic_update_slice.37
  537.8 2.2 broadcast_in_dim.152
  543.7 2.7 add_add_fusion.2
  547.5 4.0 fusion.70
  551.5 2.9 fusion.97
  554.5 1.8 fusion.96
  556.4 1.7 fusion.95
  558.2 7.4 fusion.83
  567.2 7.5 fusion.55
  574.8 262.4 %all-reduce.14.cloned.1.call-done = (f32[1024,1024]{1,0:T(8,128)}, f32[1024,1024]{1,0:T(8,128)}) async-done(((f32[1024,1024]{1,0:T(8,128)}, f32[1024,1024]{1,0:T(8,128)}), (f32[1024,1024]{1,0:T(8,128)}, f32[1024,1024]{1,0:T(8,128)})) %all-reduce.14.cloned.1.call-update) | async-done | bytes 8388624 | tf_op jit(solution)/shard_map/psum | solution.py:214
  837.2 4.8 multiply_reduce_fusion.3
  843.1 1.7 fusion.87
  846.3 2.7 fusion.71
  849.1 2.5 fusion.73
  851.6 4.1 fusion.90
  856.7 5.3 fusion.39
  862.1 3.2 broadcast_multiply_fusion
  868.5 24.1 %all-reduce.4 = (f32[256]{0:T(256)S(1)}, f32[1536]{0:T(1024)S(1)}, f32[1024]{0:T(1024)S(1)}, f32[1024]{0:T(1024)S(1)}) all-reduce(f32[256]{0:T(256)S(1)} %get-tuple-element.423, f32[1536]{0:T(1024)S(1)} %get-tuple-element.372, f32[1024]{0:T(1024)S(1)} %copy-done.52, ...), channel_id=6, replica_groups=mesh['dp'=8,'tensor'=4] {'dp'}, use_global_device_ids=true, to_apply=%region_25.26.clone | all-reduce | flops 3840 | bytes 30720
  895.0 2.7 dynamic-slice_add_fusion.2
  897.6 17.9 %reduce-scatter.23.cloned.1.call-done = f32[128,256]{1,0:T(8,128)} async-done(((f32[1024,256]{1,0:T(8,128)}), f32[128,256]{1,0:T(8,128)}) %reduce-scatter.23.cloned.1.call-update) | async-done | bytes 131088 | tf_op jit(solution)/shard_map/reduce_scatter | solution.py:299
  915.5 39.8 %reduce-scatter.21.cloned.1.call-done = f32[128,256]{1,0:T(8,128)} async-done(((f32[1024,256]{1,0:T(8,128)}), f32[128,256]{1,0:T(8,128)}) %reduce-scatter.21.cloned.1.call-update) | async-done | bytes 131088 | tf_op jit(solution)/shard_map/reduce_scatter | solution.py:298
  955.3 39.8 %reduce-scatter.19.cloned.1.call-done = f32[128,256]{1,0:T(8,128)} async-done(((f32[1024,256]{1,0:T(8,128)}), f32[128,256]{1,0:T(8,128)}) %reduce-scatter.19.cloned.1.call-update) | async-done | bytes 131088 | tf_op jit(solution)/shard_map/reduce_scatter | solution.py:297
  995.1 55.3 %reduce-scatter.27.cloned.1.call-done = f32[128,1024]{1,0:T(8,128)} async-done(((f32[1024,1024]{1,0:T(8,128)}), f32[128,1024]{1,0:T(8,128)}) %reduce-scatter.27.cloned.1.call-update) | async-done | bytes 524304 | tf_op jit(solution)/shard_map/reduce_scatter | solution.py:301
  1050.4 55.5 %reduce-scatter.29.cloned.1.call-done = f32[1024,128]{1,0:T(8,128)} async-done(((f32[1024,1024]{1,0:T(8,128)}), f32[1024,128]{1,0:T(8,128)}) %reduce-scatter.29.cloned.1.call-update) | async-done | bytes 524304 | tf_op jit(solution)/shard_map/reduce_scatter | solution.py:303
  1105.9 45.1 %reduce-scatter.15.cloned.1.call-done = f32[256,256]{1,0:T(8,128)} async-done(((f32[2048,256]{1,0:T(8,128)}), f32[256,256]{1,0:T(8,128)}) %reduce-scatter.15.cloned.1.call-update) | async-done | bytes 262160 | tf_op jit(solution)/shard_map/reduce_scatter | solution.py:293
  1151.0 79.6 %reduce-scatter.13.cloned.1.call-done = f32[1024,256]{1,0:T(8,128)} async-done(((f32[1024,1024]{1,0:T(8,128)}), f32[1024,256]{1,0:T(8,128)}) %reduce-scatter.13.cloned.1.call-update) | async-done | bytes 1048592 | tf_op jit(solution)/shard_map/reduce_scatter | solution.py:269
  1230.6 80.2 %reduce-scatter.11.cloned.1.call-done = f32[1024,256]{1,0:T(8,128)} async-done(((f32[1024,1024]{1,0:T(8,128)}), f32[1024,256]{1,0:T(8,128)}) %reduce-scatter.11.cloned.1.call-update) | async-done | bytes 1048592 | tf_op jit(solution)/shard_map/reduce_scatter | solution.py:268
  1310.8 66.5 %reduce-scatter.17.cloned.1.call-done = f32[128,1536]{1,0:T(8,128)} async-done(((f32[1024,1536]{1,0:T(8,128)}), f32[128,1536]{1,0:T(8,128)}) %reduce-scatter.17.cloned.1.call-update) | async-done | bytes 786448 | tf_op jit(solution)/shard_map/reduce_scatter | solution.py:295
  (247 shorter events, 46.1 us)
Async XLA Ops:
  7.2 8.3 copy-start
  7.2 4.7 copy-start.58
  7.2 90.8 %all-gather.4.cloned.1.call-start = ((), (), s32[]{:S(2)}) async-start(), calls=%async_computation.10 | async-start | bytes 5242880 | tf_op jit(solution)/shard_map/all_gather | solution.py:186
  7.3 2.4 copy-start.24
  7.3 4.6 copy-start.29
  9.9 2.0 copy-start.30
  11.9 4.2 copy-start.50
  11.9 4.2 copy-start.26
  14.1 275.1 %all-reduce.10.cloned.1.call-start = ((), (), s32[]{:S(2)}) async-start(), calls=%async_computation.11 | async-start | bytes 8388608 | tf_op jit(solution)/shard_map/psum | solution.py:206
  38.0 66.0 %copy-start.38 = (f32[1,1024]{1,0:T(1,128)}, f32[1,1024]{1,0:T(1,128)S(1)}, u32[]{:S(2)}) copy-start(f32[1,1024]{1,0:T(1,128)S(1)} %get-tuple-element.454) | copy-start | bytes 12292
  38.0 255.8 %copy-start.53 = (f32[1,1024]{1,0:T(1,128)}, f32[1,1024]{1,0:T(1,128)S(1)}, u32[]{:S(2)}) copy-start(f32[1,1024]{1,0:T(1,128)S(1)} %get-tuple-element.451) | copy-start | bytes 12292
  38.0 260.8 %copy-start.44 = (f32[1,1024]{1,0:T(1,128)}, f32[1,1024]{1,0:T(1,128)S(1)}, u32[]{:S(2)}) copy-start(f32[1,1024]{1,0:T(1,128)S(1)} %get-tuple-element.450) | copy-start | bytes 12292
  39.2 68.5 %copy-start.27 = (f32[1024,32]{0,1:T(8,128)}, f32[1024,32]{0,1:T(8,128)S(1)}, u32[]{:S(2)}) copy-start(f32[1024,32]{0,1:T(8,128)S(1)} %get-tuple-element.457) | copy-start | bytes 393220
  100.4 3.5 copy-start.2
  100.5 4.2 copy-start.36
  103.4 2.9 copy-start.40
  104.7 2.3 copy-start.6
  108.2 24.6 %copy-start.20 = (bf16[256,1024]{1,0:T(8,128)(2,1)S(1)}, bf16[256,1024]{1,0:T(8,128)(2,1)}, u32[]{:S(2)}) copy-start(bf16[256,1024]{1,0:T(8,128)(2,1)} %param.32) | copy-start | bytes 1572868
  112.9 2.3 copy-start.32
  124.3 2.3 copy-start.32
  132.8 2.7 copy-start.15
  135.5 328.8 %all-reduce.12.cloned.1.call-start = ((), (), s32[]{:S(2)}) async-start(), calls=%async_computation.12 | async-start | bytes 8388608 | tf_op jit(solution)/shard_map/psum | solution.py:227
  293.2 5.6 copy-start.4
  293.2 3.1 copy-start.55
  296.3 2.5 copy-start.12
  296.3 2.5 copy-start.56
  296.3 2.5 copy-start.57
  298.8 5.8 copy-start.60
  310.2 526.9 %all-reduce.14.cloned.1.call-start = ((), (), s32[]{:S(2)}) async-start(), calls=%async_computation.23 | async-start | bytes 16777216 | tf_op jit(solution)/shard_map/psum | solution.py:214
  464.3 5.3 copy-start.5
  464.3 5.9 copy-start.10
  470.3 2.2 copy-start.11
  470.3 2.9 copy-start.13
  473.1 3.4 copy-start.21
  474.5 2.1 copy-start.8
  478.1 63.2 %copy-start.28 = (f32[1024,32]{0,1:T(8,128)S(1)}, f32[1024,32]{0,1:T(8,128)}, u32[]{:S(2)}) copy-start(f32[1024,32]{0,1:T(8,128)} %copy-done.27) | copy-start | bytes 393220
  478.1 63.2 %copy-start.35 = (f32[1024,32]{0,1:T(8,128)S(1)}, f32[1024,32]{0,1:T(8,128)}, u32[]{:S(2)}) copy-start(f32[1024,32]{0,1:T(8,128)} %get-tuple-element.455) | copy-start | bytes 393220
  537.8 3.9 copy-start.22
  541.3 2.4 copy-start.19
  541.7 1.9 copy-start.17
  546.4 5.1 copy-start.7
  546.5 351.2 %reduce-scatter.25.cloned.1.call-start = ((), (), s32[]{:S(2)}) async-start(), calls=%async_computation.20 | async-start | bytes 1179648 | tf_op jit(solution)/shard_map/reduce_scatter | solution.py:300
  551.4 3.1 copy-start.18
  551.5 364.1 %reduce-scatter.23.cloned.1.call-start = ((), (), s32[]{:S(2)}) async-start(), calls=%async_computation.19 | async-start | bytes 1179648 | tf_op jit(solution)/shard_map/reduce_scatter | solution.py:299
  554.5 400.9 %reduce-scatter.21.cloned.1.call-start = ((), (), s32[]{:S(2)}) async-start(), calls=%async_computation.18 | async-start | bytes 1179648 | tf_op jit(solution)/shard_map/reduce_scatter | solution.py:298
  556.3 1.9 copy-start.54
  556.3 438.8 %reduce-scatter.19.cloned.1.call-start = ((), (), s32[]{:S(2)}) async-start(), calls=%async_computation.17 | async-start | bytes 1179648 | tf_op jit(solution)/shard_map/reduce_scatter | solution.py:297
  558.1 492.3 %reduce-scatter.27.cloned.1.call-start = ((), (), s32[]{:S(2)}) async-start(), calls=%async_computation.21 | async-start | bytes 4718592 | tf_op jit(solution)/shard_map/reduce_scatter | solution.py:301
  565.6 1.6 copy-start.45
  565.6 540.2 %reduce-scatter.29.cloned.1.call-start = ((), (), s32[]{:S(2)}) async-start(), calls=%async_computation.22 | async-start | bytes 4718592 | tf_op jit(solution)/shard_map/reduce_scatter | solution.py:303
  574.7 262.5 %copy-start.37 = (f32[1024]{0:T(1024)S(1)}, f32[1024]{0:T(1024)}, u32[]{:S(2)}) copy-start(f32[1024]{0:T(1024)} %copy-done.36) | copy-start | bytes 12292
  574.7 262.5 %copy-start.39 = (f32[1,1024]{1,0:T(1,128)S(1)}, f32[1,1024]{1,0:T(1,128)}, u32[]{:S(2)}) copy-start(f32[1,1024]{1,0:T(1,128)} %copy-done.38) | copy-start | bytes 12292
  574.7 262.5 %copy-start.41 = (f32[1024]{0:T(1024)S(1)}, f32[1024]{0:T(1024)}, u32[]{:S(2)}) copy-start(f32[1024]{0:T(1024)} %copy-done.40) | copy-start | bytes 12292
  574.7 576.3 %reduce-scatter.15.cloned.1.call-start = ((), (), s32[]{:S(2)}) async-start(), calls=%async_computation.15 | async-start | bytes 2359296 | tf_op jit(solution)/shard_map/reduce_scatter | solution.py:293
  837.1 4.8 copy-start.43
  837.2 4.8 copy-start.3
  837.2 5.9 copy-start.9
  843.1 3.2 copy-start.31
  849.0 381.6 %reduce-scatter.13.cloned.1.call-start = ((), (), s32[]{:S(2)}) async-start(), calls=%async_computation.14 | async-start | bytes 5242880 | tf_op jit(solution)/shard_map/reduce_scatter | solution.py:269
  855.8 455.0 %reduce-scatter.11.cloned.1.call-start = ((), (), s32[]{:S(2)}) async-start(), calls=%async_computation.13 | async-start | bytes 5242880 | tf_op jit(solution)/shard_map/reduce_scatter | solution.py:268
  856.5 520.7 %reduce-scatter.17.cloned.1.call-start = ((), (), s32[]{:S(2)}) async-start(), calls=%async_computation.16 | async-start | bytes 7077888 | tf_op jit(solution)/shard_map/reduce_scatter | solution.py:295
  856.7 5.4 copy-start.49
  865.3 3.2 copy-start.52
  865.3 512.0 %copy-start.1 = (bf16[1024,1536]{1,0:T(8,128)(2,1)S(1)}, bf16[1024,1536]{1,0:T(8,128)(2,1)}, u32[]{:S(2)}) copy-start(bf16[1024,1536]{1,0:T(8,128)(2,1)} %param.27) | copy-start | bytes 9437188
  (14 other events, 14.1 us)
Sparse Core Ops, SparseCore 0:
  14.2 83.7 all-gather.3
  135.6 153.4 all-reduce.9
  310.3 153.9 all-reduce.11
  546.6 290.5 all-reduce.13
  840.7 35.0 reduce-scatter.24
  879.5 36.0 reduce-scatter.22
  919.3 35.9 reduce-scatter.20
  959.1 35.9 reduce-scatter.18
  999.0 51.2 reduce-scatter.26
  1054.5 51.3 reduce-scatter.28
  1109.7 41.2 reduce-scatter.14
  1153.8 76.7 reduce-scatter.12
  1233.5 77.2 reduce-scatter.10
  1315.0 62.2 reduce-scatter.16
where the time goes:
time: 1390 us; the launch traced here: 1380 us
  waiting for transfers between devices  1100 us (79%)
  matrix products  101 us (7%)
  local copies, waits for them, and re-layouts  59.1 us (4%)
  other arithmetic  53.8 us (4%)
  blocking collectives  40.5 us (3%)
  between operations  17.6 us (1%)
    psum x1, waiting for transfers between devices, per_device(): ffn = lax.psum(ffn_term, 'tensor') + b_down  262 us
    psum x1, waiting for transfers between devices, per_device(): lax.psum(jnp.dot(attended_flat, w_out, preferred_element_type=jnp.float32...  153 us
    psum x1, waiting for transfers between devices, per_device(): lax.psum(jnp.einsum('tf,df->td', grad_pre, w_up, preferred_element_type=j...  146 us
    reduce_scatter x1, waiting for transfers between devices, per_device(): lax.psum_scatter(grad_joined[:, :width], 'tensor', scatter_dimension=1, t...  80.2 us
    reduce_scatter x1, waiting for transfers between devices, per_device(): lax.psum_scatter(grad_joined[:, width:], 'tensor', scatter_dimension=1, t...  79.6 us
    reduce_scatter x1, waiting for transfers between devices, per_device(): lax.psum_scatter(grad_w_mod, 'dp', scatter_dimension=0, tiled=True)  66.5 us
    all_gather x1, waiting for transfers between devices, per_device(): lax.all_gather(skip_part, 'tensor', axis=1, tiled=True)  58.8 us
    reduce_scatter x1, waiting for transfers between devices, per_device(): lax.psum_scatter(grad_w_down, 'dp', scatter_dimension=1, tiled=True)  55.5 us
  transfers between devices with their start and end apart: 14, of which 13 were waited for; matrix products, arithmetic and copies ran while one was open for 5% of the time, Pallas kernels for 0%

commit v1 on v0

v1 whole, which is shorter than its diff:
```python
import functools
import math

import jax
import jax.numpy as jnp
from jax import lax
from jax.experimental import pallas as pl
from jax.experimental.pallas import tpu as pltpu
from jax.sharding import PartitionSpec as P

HEAD_DIM = 64
EPS = 1e-06
F32 = jnp.float32
BF16 = jnp.bfloat16
MESH = pl.DeviceIdType.MESH
ANY = pl.BlockSpec(memory_space=pl.ANY)
VMEM = pl.BlockSpec(memory_space=pltpu.VMEM)
GROUP = 8
NT = (((1,), (1,)), ((), ()))
NN = (((1,), (0,)), ((), ()))


def dot(a, b, dims=NN, precision=None):
    return lax.dot_general(a, b, dims, precision=precision, preferred_element_type=F32)


def remote(src, dst, send, recv, device):
    return pltpu.make_async_remote_copy(
        src_ref=src,
        dst_ref=dst,
        send_sem=send,
        recv_sem=recv,
        device_id=device,
        device_id_type=MESH,
    )


def gather_kernel(chunks, nz, *refs):
    n = len(chunks)
    (p_skip, p_qkv, p_o, p_up, p_dn, own_skip, own_small) = refs[:7]
    (o_skip, o_qkv, o_o, o_up, o_dn, o_small) = refs[7:13]
    zs, zr, ps, pr, ls = refs[13:]
    dp = lax.axis_index("dp")
    z = lax.axis_index("tensor")
    p = lax.rem(dp, GROUP)
    core = lax.rem(dp, 2)
    xb = lax.rem(dp // 2, 2)
    yb = lax.rem(dp // 4, 2)
    ds_ = 1 - 2 * core
    dx = 2 - 4 * xb
    dy = 4 - 8 * yb
    d1 = dy + core * (dx - dy)
    d2 = dx + core * (dy - dx)
    near = {1: (dp + d1, z), 2: (dp + d2, z), 3: (dp + ds_, z)}
    far = {k: (dp, lax.rem(z + nz - k, nz)) for k in range(1, nz)}
    bar = pltpu.get_barrier_semaphore()
    for device in list(near.values()) + list(far.values()):
        pl.semaphore_signal(bar, inc=1, device_id=device, device_id_type=MESH)
    pl.semaphore_wait(bar, 3 + nz - 1)
    pieces = {"skip": p_skip, "qkv": p_qkv, "o": p_o, "up": p_up, "dn": p_dn}
    outs = {"skip": o_skip, "qkv": o_qkv, "o": o_o, "up": o_up, "dn": o_dn}

    def src(ch):
        name, a, off, r = ch
        if name == "qkv":
            return pieces[name].at[a]
        return pieces[name].at[pl.ds(off, r)]

    def view(ch, k, q, zz):
        name, a, off, r = ch
        if name == "skip":
            width = p_skip.shape[1]
            return o_skip.at[pl.ds(q * p_skip.shape[0] + off, r), pl.ds(zz * width, width)]
        if name == "qkv":
            r = p_qkv.shape[1]
            return o_qkv.at[k - 1, a, pl.ds(q * r, r)]
        return outs[name].at[k - 1, pl.ds(q * pieces[name].shape[0] + off, r)]

    kk = nz - 1
    local = [
        lambda: pltpu.make_async_copy(
            own_skip, o_skip.at[:, pl.ds(z * own_skip.shape[1], own_skip.shape[1])], ls.at[0]
        ),
        lambda: pltpu.make_async_copy(own_small, o_small.at[z], ls.at[1]),
    ]

    def small(k, zz):
        return remote(own_small, o_small.at[zz], zs.at[n, k - 1], zr.at[n, k - 1], far[k])

    def zcopy(i, k, zz):
        return remote(
            src(chunks[i]),
            view(chunks[i], k, p, zz),
            zs.at[i, k - 1],
            zr.at[i, k - 1],
            far[k],
        )

    stages = {
        1: ([p], d1, 0),
        2: ([p, p + d1], d2, 1),
        3: ([p, p + d1, p + d2, p + d1 + d2], ds_, 3),
    }

    def copies(i, stage, inward):
        qs, shift, base = stages[stage]
        out = []
        for j, q in enumerate(qs):
            if inward:
                q = q + shift
            for k in range(1, nz):
                ref = view(chunks[i], k, q, lax.rem(z + k, nz))
                s = (base + j) * kk + k - 1
                out.append(remote(ref, ref, ps.at[i, s], pr.at[i, s], near[stage]))
        return out

    for c in local:
        c().start()
    for k in range(1, nz):
        small(k, z).start()
    for t in range(n + 4):
        if t < n:
            for k in range(1, nz):
                zcopy(t, k, z).start()
        if 0 <= t - 1 < n:
            for k in range(1, nz):
                zcopy(t - 1, k, lax.rem(z + k, nz)).wait_recv()
            for c in copies(t - 1, 1, False):
                c.start()
        for stage in (2, 3):
            if 0 <= t - stage < n:
                for c in copies(t - stage, stage - 1, True):
                    c.wait_recv()
                for c in copies(t - stage, stage, False):
                    c.start()
        if 0 <= t - 4 < n:
            for c in copies(t - 4, 3, True):
                c.wait_recv()
    for i in range(n):
        for k in range(1, nz):
            zcopy(i, k, z).wait_send()
        for stage in (1, 2, 3):
            for c in copies(i, stage, False):
                c.wait_send()
    for k in range(1, nz):
        small(k, z).wait_send()
        small(k, lax.rem(z + k, nz)).wait_recv()
    for c in local:
        c().wait()


def gather(p_skip, p_qkv, p_o, p_up, p_dn, own_skip, own_small, nz):
    chunks = []

    def rows(name, arr, parts):
        r = arr.shape[0] // parts
        for j in range(parts):
            chunks.append((name, 0, j * r, r))

    rows("skip", p_skip, 2)
    for a in range(3):
        chunks.append(("qkv", a, 0, 0))
    rows("o", p_o, 1)
    rows("up", p_up, 4)
    rows("dn", p_dn, 4)
    n = len(chunks)
    sd = jax.ShapeDtypeStruct
    kk = nz - 1
    outs = [
        sd((p_skip.shape[0] * GROUP, p_skip.shape[1] * nz), F32),
        sd((kk, 3, p_qkv.shape[1] * GROUP, p_qkv.shape[2]), F32),
        sd((kk, p_o.shape[0] * GROUP, p_o.shape[1]), F32),
        sd((kk, p_up.shape[0] * GROUP, p_up.shape[1]), F32),
        sd((kk, p_dn.shape[0] * GROUP, p_dn.shape[1]), F32),
        sd((nz,) + own_small.shape, F32),
    ]
    dma = pltpu.SemaphoreType.DMA
    return pl.pallas_call(
        functools.partial(gather_kernel, chunks, nz),
        out_shape=outs,
        in_specs=[ANY] * 7,
        out_specs=[ANY] * 6,
        scratch_shapes=[dma((n + 1, kk)), dma((n + 1, kk)), dma((n, 7 * kk)), dma((n, 7 * kk)), dma((2,))],
        compiler_params=pltpu.CompilerParams(collective_id=0, has_side_effects=True),
    )(p_skip, p_qkv, p_o, p_up, p_dn, own_skip, own_small)


def reduce_kernel(ndp, nz, na, *refs):
    bits = ndp.bit_length() - 1
    ins = refs[:na]
    small, part = refs[na : na + 2]
    outs = refs[na + 2 : 2 * na + 2]
    all_small, all_part = refs[2 * na + 2 : 2 * na + 4]
    rest = refs[2 * na + 4 :]
    recv0, lev0 = rest[:na], rest[na : 2 * na]
    half_refs = rest[2 * na : -8]
    gz, s_send, s_recv, q_send, q_recv, z_send, z_recv, l_sem = rest[-8:]
    dp = lax.axis_index("dp")
    z = lax.axis_index("tensor")
    mine = [lax.rem(dp // (1 << b), 2) for b in range(bits)]
    partner = [(dp + (1 << b) * (1 - 2 * mine[b]), z) for b in range(bits)]
    bar = pltpu.get_barrier_semaphore()

    def others(j):
        return lax.rem(dp + j, ndp)

    for j in range(1, ndp):
        pl.semaphore_signal(bar, inc=1, device_id=(others(j), z), device_id_type=MESH)
    for k in range(1, nz):
        pl.semaphore_signal(bar, inc=1, device_id=(dp, lax.rem(z + k, nz)), device_id_type=MESH)
    pl.semaphore_wait(bar, ndp - 1 + nz - 1)

    def gzc(k, zz):
        return remote(part, gz.at[zz], z_send.at[k - 1], z_recv.at[k - 1], (dp, lax.rem(z + nz - k, nz)))

    for k in range(1, nz):
        gzc(k, z).start()

    def first(a, i):
        s = 2 * i + 1 - mine[0]
        return remote(ins[a].at[s], recv0[a].at[i], s_send.at[a, i], s_recv.at[a, i], partner[0])

    for a in range(na):
        for i in range(ndp // 2):
            first(a, i).start()
    gz[z] = part[...]

    def sml(j, row):
        return remote(small, all_small.at[row], q_send.at[0, j - 1], q_recv.at[0, j - 1], (others(j), z))

    def prt(j, row):
        return remote(gz, all_part.at[row], q_send.at[1, j - 1], q_recv.at[1, j - 1], (others(j), z))

    own = [
        lambda: pltpu.make_async_copy(small, all_small.at[dp], l_sem.at[0]),
        lambda: pltpu.make_async_copy(gz, all_part.at[dp], l_sem.at[1]),
    ]
    for j in range(1, ndp):
        sml(j, dp).start()
    own[0]().start()
    for k in range(1, nz):
        gzc(k, lax.rem(z + k, nz)).wait_recv()
    for j in range(1, ndp):
        prt(j, dp).start()
    own[1]().start()
    for a in range(na):
        for i in range(ndp // 2):
            first(a, i).wait_recv()
            lev0[a][i] = ins[a][2 * i + mine[0]] + recv0[a][i]
    orders = [list(range(1, bits)), list(range(bits - 1, 0, -1))]
    state = {}
    pos = 0
    for a in range(na):
        for h in range(2):
            cw = ins[a].shape[2] // 2
            state[a, h] = (lev0[a].at[:, :, pl.ds(h * cw, cw)], list(range(1, bits)))
    pending = []
    for step in range(bits - 1):
        todo = []
        for a in range(na):
            for h in range(2):
                src, free = state[a, h]
                b = orders[h][step]
                at = free.index(b)
                lo = 1 << at
                left = [f for f in free if f != b]
                cnt = 1 << len(left)
                recv, out = half_refs[pos], half_refs[pos + 1]
                sem_s, sem_r = half_refs[pos + 2], half_refs[pos + 3]
                pos += 4
                items = []
                for i in range(cnt):
                    base = (i // lo) * 2 * lo + i % lo
                    keep = base + lo * mine[b]
                    give = base + lo * (1 - mine[b])
                    c = functools.partial(
                        remote, src.at[give], recv.at[i], sem_s.at[i], sem_r.at[i], partner[b]
                    )
                    c().start()
                    items.append((c, keep, i))
                todo.append((a, h, src, recv, out, items))
                state[a, h] = (out, left)
        for a, h, src, recv, out, items in todo:
            cw = ins[a].shape[2] // 2
            for c, keep, i in items:
                c().wait_recv()
                if step == bits - 2:
                    outs[a][:, pl.ds(h * cw, cw)] = src[keep] + recv[i]
                else:
                    out[i] = src[keep] + recv[i]
                pending.append(c)
    for c in pending:
        c().wait_send()
    for a in range(na):
        for i in range(ndp // 2):
            first(a, i).wait_send()
    for k in range(1, nz):
        gzc(k, z).wait_send()
    for j in range(1, ndp):
        sml(j, dp).wait_send()
        prt(j, dp).wait_send()
        row = lax.rem(dp + ndp - j, ndp)
        sml(j, row).wait_recv()
        prt(j, row).wait_recv()
    for c in own:
        c().wait()


def reduce_over_dp(arrays, small, part, ndp, nz, cid):
    na = len(arrays)
    bits = ndp.bit_length() - 1
    sd = jax.ShapeDtypeStruct
    dma = pltpu.SemaphoreType.DMA
    scratch = [pltpu.VMEM((ndp // 2,) + a.shape[1:], F32) for a in arrays] * 2
    for step in range(bits - 1):
        cnt = ndp >> (step + 2)
        for a in arrays:
            for h in range(2):
                shape = (cnt, a.shape[1], a.shape[2] // 2)
                scratch += [pltpu.VMEM(shape, F32), pltpu.VMEM(shape, F32), dma((cnt,)), dma((cnt,))]
    scratch += [
        pltpu.VMEM((nz,) + part.shape, F32),
        dma((na, ndp // 2)),
        dma((na, ndp // 2)),
        dma((2, ndp - 1)),
        dma((2, ndp - 1)),
        dma((nz - 1,)),
        dma((nz - 1,)),
        dma((2,)),
    ]
    return pl.pallas_call(
        functools.partial(reduce_kernel, ndp, nz, na),
        out_shape=[sd(a.shape[1:], F32) for a in arrays]
        + [sd((ndp,) + small.shape, F32), sd((ndp, nz) + part.shape, F32)],
        in_specs=[VMEM] * (na + 2),
        out_specs=[VMEM] * (na + 2),
        scratch_shapes=scratch,
        compiler_params=pltpu.CompilerParams(
            collective_id=cid, has_side_effects=True, vmem_limit_bytes=56 << 20
        ),
    )(*arrays, small, part)


def swap_halves(u):
    n = u.shape[1]
    lane = lax.broadcasted_iota(jnp.int32, u.shape, 1)
    half = HEAD_DIM // 2
    return jnp.where(
        lane % HEAD_DIM < half, pltpu.roll(u, n - half, 1), pltpu.roll(u, half, 1)
    )


def qkv_kernel(x_ref, wq_ref, wk_ref, wv_ref, w_ref, cos_ref, sin_ref, q_ref, k_ref, v_ref):
    g = pl.program_id(0)
    own = (wq_ref, wk_ref, wv_ref)
    outs = (q_ref, k_ref, v_ref)

    def run(weights):
        x = x_ref[...]
        for a in range(3):
            u = dot(x, weights[a])
            if a < 2:
                u = u * cos_ref[...] + swap_halves(u) * sin_ref[...]
            u = u.astype(BF16)
            if a == 0:
                u = u * (HEAD_DIM**-0.5)
            outs[a][...] = u

    @pl.when(g == 0)
    def _():
        run([w[...] for w in own])

    @pl.when(g > 0)
    def _():
        run([w_ref[0, a].astype(BF16) for a in range(3)])


def qkv(x, wq, wk, wv, w, cos, sin):
    t, d = x.shape
    e = wq.shape[1]
    groups = w.shape[0] + 1
    full = lambda s: pl.BlockSpec(s, lambda g: (0, 0))
    out = jax.ShapeDtypeStruct((t, groups * e), BF16)
    return pl.pallas_call(
        qkv_kernel,
        grid=(groups,),
        out_shape=[out] * 3,
        in_specs=[full((t, d))]
        + [full((d, e))] * 3
        + [pl.BlockSpec((1, 3, d, e), lambda g: (jnp.maximum(g - 1, 0), 0, 0, 0))]
        + [full((t, e))] * 2,
        out_specs=[pl.BlockSpec((t, e), lambda g: (0, g))] * 3,
        compiler_params=pltpu.CompilerParams(vmem_limit_bytes=56 << 20),
    )(x, wq, wk, wv, w, cos, sin)


QB = 256
KB = 128
NEG = -1e30


def head_mask(shape, h):
    lane = lax.broadcasted_iota(jnp.int32, shape, 1)
    return (lane // HEAD_DIM) == h


def attn_fwd_kernel(heads, lo_ref, hi_ref, q_ref, k_ref, v_ref, segq_ref, segk_ref, o_ref, lse_ref, vt_ref):
    i = pl.program_id(1)

    @pl.when(i == 0)
    def _():
        vt_ref[...] = v_ref[...].T

    q = q_ref[...]
    qm = [jnp.where(head_mask(q.shape, h), q, jnp.zeros_like(q)) for h in range(heads)]
    segq = segq_ref[0, pl.ds(0, 1)]
    rows = q.shape[0]

    def body(j, carry):
        ms, ls, os_ = carry
        start = pl.multiple_of(j * KB, KB)
        kb = k_ref[pl.ds(start, KB), :]
        segk = segk_ref[pl.ds(start, KB), :]
        same = jnp.concatenate([segk] * (rows // 128), axis=1) == segq
        nm, nl, no = [], [], []
        for h in range(heads):
            s = jnp.where(same, dot(kb, qm[h], NT), NEG)
            m = jnp.maximum(ms[h], jnp.max(s, axis=0, keepdims=True))
            alpha = jnp.exp(ms[h] - m)
            p = jnp.exp(s - m)
            nl.append(ls[h] * alpha + jnp.sum(p, axis=0, keepdims=True))
            vt = vt_ref[pl.ds(h * HEAD_DIM, HEAD_DIM), pl.ds(start, KB)]
            no.append(os_[h] * alpha + dot(vt, p.astype(BF16)))
            nm.append(m)
        return nm, nl, no

    init = (
        [jnp.full((1, rows), NEG, F32)] * heads,
        [jnp.zeros((1, rows), F32)] * heads,
        [jnp.zeros((HEAD_DIM, rows), F32)] * heads,
    )
    ms, ls, os_ = lax.fori_loop(lo_ref[i], hi_ref[i], body, init)
    out = jnp.concatenate([os_[h] / ls[h] for h in range(heads)], axis=0)
    o_ref[...] = out.T.astype(BF16)
    lse = [ms[h] + jnp.log(ls[h]) for h in range(heads)]
    lse_ref[0] = jnp.concatenate(lse + [jnp.zeros((8 - heads, rows), F32)], axis=0)


def attn_fwd(q, k, v, seg_row, seg_col, lo, hi, groups):
    t = q.shape[0]
    e = q.shape[1] // groups
    heads = e // HEAD_DIM
    return pl.pallas_call(
        functools.partial(attn_fwd_kernel, heads),
        out_shape=[
            jax.ShapeDtypeStruct(q.shape, BF16),
            jax.ShapeDtypeStruct((groups, 8, t), F32),
        ],
        grid_spec=pltpu.PrefetchScalarGridSpec(
            num_scalar_prefetch=2,
            grid=(groups, t // QB),
            in_specs=[
                pl.BlockSpec((QB, e), lambda g, i, *_: (i, g)),
                pl.BlockSpec((t, e), lambda g, i, *_: (0, g)),
                pl.BlockSpec((t, e), lambda g, i, *_: (0, g)),
                pl.BlockSpec((1, 8, QB), lambda g, i, *_: (0, 0, i)),
                pl.BlockSpec((t, 128), lambda g, i, *_: (0, 0)),
            ],
            out_specs=[
                pl.BlockSpec((QB, e), lambda g, i, *_: (i, g)),
                pl.BlockSpec((1, 8, QB), lambda g, i, *_: (g, 0, i)),
            ],
            scratch_shapes=[pltpu.VMEM((e, t), BF16)],
        ),
        compiler_params=pltpu.CompilerParams(vmem_limit_bytes=48 << 20),
    )(lo, hi, q, k, v, seg_row, seg_col)


def attn_bwd_kernel(
    heads,
    lo_ref,
    hi_ref,
    q_ref,
    k_ref,
    v_ref,
    att_ref,
    g_ref,
    lse_ref,
    segq_ref,
    segk_ref,
    cos_ref,
    sin_ref,
    gq_ref,
    gk_ref,
    gv_ref,
    kt_ref,
    dk_ref,
    dv_ref,
):
    t, e = k_ref.shape
    kt_ref[...] = k_ref[...].T
    dk_ref[...] = jnp.zeros_like(dk_ref)
    dv_ref[...] = jnp.zeros_like(dv_ref)
    row = lax.broadcasted_iota(jnp.int32, (8, e), 0)
    lane = lax.broadcasted_iota(jnp.int32, (8, e), 1)
    ind = jnp.where(lane // HEAD_DIM == row, 1.0, 0.0).astype(F32)

    @pl.loop(0, t // QB)
    def _(i):
        qs = pl.multiple_of(i * QB, QB)
        q = q_ref[pl.ds(qs, QB), :]
        g = g_ref[pl.ds(qs, QB), :]
        zero = jnp.zeros_like(q)
        qm = [jnp.where(head_mask(q.shape, h), q, zero) for h in range(heads)]
        gm = [jnp.where(head_mask(q.shape, h), g, zero) for h in range(heads)]
        segq = segq_ref[0, pl.ds(0, 1), pl.ds(qs, QB)]
        prod = g.astype(F32) * att_ref[pl.ds(qs, QB), :].astype(F32)
        delta = dot(ind, prod, NT, lax.Precision.HIGHEST)
        lse = lse_ref[0, :, pl.ds(qs, QB)]

        def body(j, dq):
            start = pl.multiple_of(j * KB, KB)
            kb = k_ref[pl.ds(start, KB), :]
            vb = v_ref[pl.ds(start, KB), :]
            segk = segk_ref[pl.ds(start, KB), :]
            same = jnp.concatenate([segk] * (QB // 128), axis=1) == segq
            ndq = []
            dk = dk_ref[pl.ds(start, KB), :]
            dv = dv_ref[pl.ds(start, KB), :]
            for h in range(heads):
                s = jnp.where(same, dot(kb, qm[h], NT), NEG)
                p = jnp.exp(s - lse[h : h + 1])
                dp_ = dot(vb, gm[h], NT)
                ds = (p * (dp_ - delta[h : h + 1])).astype(BF16)
                dv = dv + dot(p.astype(BF16), gm[h])
                dk = dk + dot(ds, qm[h])
                kt = kt_ref[pl.ds(h * HEAD_DIM, HEAD_DIM), pl.ds(start, KB)]
                ndq.append(dq[h] + dot(kt, ds))
            dk_ref[pl.ds(start, KB), :] = dk
            dv_ref[pl.ds(start, KB), :] = dv
            return ndq

        dq = lax.fori_loop(
            lo_ref[i], hi_ref[i], body, [jnp.zeros((HEAD_DIM, QB), F32)] * heads
        )
        dqf = jnp.concatenate(dq, axis=0).T * (HEAD_DIM**-0.5)
        cos = cos_ref[pl.ds(qs, QB), :]
        sin = sin_ref[pl.ds(qs, QB), :]
        gq_ref[pl.ds(qs, QB), :] = (dqf * cos - swap_halves(dqf) * sin).astype(BF16)

    dk = dk_ref[...]
    gk_ref[...] = (dk * cos_ref[...] - swap_halves(dk) * sin_ref[...]).astype(BF16)
    gv_ref[...] = dv_ref[...].astype(BF16)


def attn_bwd(q, k, v, att, g, lse, seg_row, seg_col, lo, hi, cos, sin, groups):
    t = q.shape[0]
    e = q.shape[1] // groups
    heads = e // HEAD_DIM
    col = pl.BlockSpec((t, e), lambda g, *_: (0, g))
    full = lambda s: pl.BlockSpec(s, lambda g, *_: (0, 0))
    return pl.pallas_call(
        functools.partial(attn_bwd_kernel, heads),
        out_shape=[jax.ShapeDtypeStruct(q.shape, BF16)] * 3,
        grid_spec=pltpu.PrefetchScalarGridSpec(
            num_scalar_prefetch=2,
            grid=(groups,),
            in_specs=[col] * 5
            + [
                pl.BlockSpec((1, 8, t), lambda g, *_: (g, 0, 0)),
                pl.BlockSpec((1, 8, t), lambda g, *_: (0, 0, 0)),
                full((t, 128)),
                full((t, e)),
                full((t, e)),
            ],
            out_specs=[col] * 3,
            scratch_shapes=[
                pltpu.VMEM((e, t), BF16),
                pltpu.VMEM((t, e), F32),
                pltpu.VMEM((t, e), F32),
            ],
        ),
        compiler_params=pltpu.CompilerParams(vmem_limit_bytes=56 << 20),
    )(lo, hi, q, k, v, att, g, lse, seg_row, seg_col, cos, sin)


def gnormed_kernel(gq_ref, gk_ref, gv_ref, wq_ref, wk_ref, wv_ref, w_ref, o_ref):
    g = pl.program_id(0)
    grads = (gq_ref, gk_ref, gv_ref)
    own = (wq_ref, wk_ref, wv_ref)

    @pl.when(g == 0)
    def _():
        o_ref[...] = dot(gq_ref[...], wq_ref[...], NT)
        for a in (1, 2):
            o_ref[...] += dot(grads[a][...], own[a][...], NT)

    @pl.when(g > 0)
    def _():
        for a in range(3):
            o_ref[...] += dot(grads[a][...], w_ref[0, a].astype(BF16), NT)


def gnormed(gq, gk, gv, wq, wk, wv, w):
    t = gq.shape[0]
    d, e = wq.shape
    groups = w.shape[0] + 1
    full = lambda s: pl.BlockSpec(s, lambda g: (0, 0))
    return pl.pallas_call(
        gnormed_kernel,
        grid=(groups,),
        out_shape=jax.ShapeDtypeStruct((t, d), F32),
        in_specs=[pl.BlockSpec((t, e), lambda g: (0, g))] * 3
        + [full((d, e))] * 3
        + [pl.BlockSpec((1, 3, d, e), lambda g: (jnp.maximum(g - 1, 0), 0, 0, 0))],
        out_specs=full((t, d)),
        compiler_params=pltpu.CompilerParams(vmem_limit_bytes=56 << 20),
    )(gq, gk, gv, wq, wk, wv, w)


def stats(values):
    mean_val = jnp.mean(values, axis=-1, keepdims=True)
    centred = values - mean_val
    r = lax.rsqrt(jnp.mean(centred * centred, axis=-1, keepdims=True) + EPS)
    return centred * r, r


def norm_pull(x, r, scale, grad):
    gp = grad * (1.0 + scale)
    return r * (
        gp - jnp.mean(gp, axis=-1, keepdims=True) - x * jnp.mean(gp * x, axis=-1, keepdims=True)
    )


def time_freqs(width):
    half = width // 2
    return jnp.exp(-math.log(10000.0) * jnp.arange(half, dtype=F32) / half)


def time_embed(flow_time, width):
    angles = 1000.0 * flow_time[:, None] * time_freqs(width)[None, :]
    both = jnp.concatenate([jnp.cos(angles), jnp.sin(angles)], axis=1)
    return jax.nn.silu(both).astype(BF16)


def gelu_parts(v):
    c = math.sqrt(2.0 / math.pi)
    v2 = v * v
    th = jnp.tanh(c * v * (1.0 + 0.044715 * v2))
    act = 0.5 * v * (1.0 + th)
    slope = 0.5 * (1.0 + th) + (0.5 * c) * v * (1.0 - th * th) * (1.0 + 3.0 * 0.044715 * v2)
    return act, slope


def per_device(ndp, nz, *args):
    (
        frames,
        skip_in,
        flow_time,
        segment_ids,
        w_skip,
        b_skip,
        w_mod,
        b_mod,
        w_q,
        w_k,
        w_v,
        w_o,
        w_up,
        b_up,
        w_dn,
        b_dn,
        out_grad,
    ) = args
    t, d = frames.shape
    loc = w_q.shape[1]
    fl = w_up.shape[1]
    dp = lax.axis_index("dp")
    z = lax.axis_index("tensor")
    p = dp % GROUP

    def piece(w):
        r = w.shape[0] // GROUP
        return lax.dynamic_slice_in_dim(w, p * r, r, 0).astype(F32)

    embed = time_embed(flow_time, d)
    mod_part = dot(embed, w_mod)[0] + b_mod
    own_small = jnp.concatenate([mod_part, b_skip, b_up])[None, :]
    wskip, wqkv, wo, wup, wdn, small = gather(
        piece(w_skip),
        jnp.stack([piece(w_q), piece(w_k), piece(w_v)]),
        piece(w_o),
        piece(w_up),
        piece(w_dn),
        w_skip.astype(F32),
        own_small,
        nz,
    )
    small = small[:, 0]
    nm = mod_part.shape[0]
    mod = small[:, :nm].reshape(6, d)
    shift1, scale1, gate1, shift2, scale2, gate2 = [mod[i][None, :] for i in range(6)]
    bskip = small[:, nm : nm + loc].reshape(1, d)
    bup = [
        lax.dynamic_index_in_dim(small[:, nm + loc :], (z + k) % nz, 0, keepdims=True)
        for k in range(nz)
    ]
    up = [w_up] + [wup[k].astype(BF16) for k in range(nz - 1)]
    dn = [w_dn] + [wdn[k].astype(BF16) for k in range(nz - 1)]
    wo_all = [w_o] + [wo[k].astype(BF16) for k in range(nz - 1)]

    def own_cols(a):
        return lax.dynamic_slice_in_dim(a, z * loc, loc, a.ndim - 1)

    seg = segment_ids[0]
    idx = jnp.arange(t, dtype=jnp.int32)
    nseg = 4
    starts = jnp.stack([jnp.sum((seg < s).astype(jnp.int32)) for s in range(nseg + 1)])
    first = jnp.zeros_like(seg)
    for s in range(1, nseg):
        first = jnp.where(seg >= s, starts[s], first)
    pos = (idx - first).astype(F32)
    half = HEAD_DIM // 2
    inv = jnp.exp(-math.log(10000.0) * 2.0 * jnp.arange(half, dtype=F32) / HEAD_DIM)
    ang = pos[:, None] * inv[None, :]
    cos_h, sin_h = jnp.cos(ang), jnp.sin(ang)
    cos = jnp.tile(cos_h, (1, loc // half))
    sin = jnp.tile(jnp.concatenate([-sin_h, sin_h], axis=1), (1, loc // HEAD_DIM))
    qb_first, qb_last = seg[::QB], seg[QB - 1 :: QB]
    lo = jnp.take(starts, qb_first) // KB
    hi = (jnp.take(starts, qb_last + 1) + KB - 1) // KB
    seg_row = jnp.broadcast_to(seg[None, None, :], (1, 8, t))
    seg_col = jnp.broadcast_to(seg[:, None], (t, 128))

    hidden = (
        dot(frames, wskip[:d].astype(BF16)) + dot(skip_in, wskip[d:].astype(BF16)) + bskip
    )
    x1, r1 = stats(hidden)
    normed = (x1 * (1.0 + scale1) + shift1).astype(BF16)
    q, k, v = qkv(normed, w_q, w_k, w_v, wqkv, cos, sin)
    att, lse = attn_fwd(q, k, v, seg_row, seg_col, lo, hi, nz)
    branch = sum(dot(att[:, i * loc : (i + 1) * loc], wo_all[i]) for i in range(nz))
    mid = hidden + gate1 * branch
    x2, r2 = stats(mid)
    normed2 = (x2 * (1.0 + scale2) + shift2).astype(BF16)
    g_out = out_grad.astype(F32)
    g_ffn = (gate2 * g_out).astype(BF16)
    ffn_own = own_cols(b_dn)[None, :]
    g_normed2 = 0.0
    for i in range(nz):
        pre = dot(normed2, up[i]) + bup[i]
        act, slope = gelu_parts(pre)
        act = act.astype(BF16)
        ffn_own = ffn_own + dot(act, own_cols(dn[i]))
        g_pre = (dot(g_ffn, dn[i], NT) * slope).astype(BF16)
        g_normed2 = g_normed2 + dot(g_pre, up[i], NT)
        if i == 0:
            act_own, g_pre_own = act, g_pre
    output = own_cols(mid) + own_cols(gate2) * ffn_own
    g_gate2_own = jnp.sum(own_cols(g_out) * ffn_own, axis=0)
    g_b_dn = gate2[0] * jnp.sum(g_out, axis=0)
    tn = (((0,), (0,)), ((), ()))
    g_w_up = dot(normed2, g_pre_own, tn)
    g_w_dn_t = dot(g_ffn, act_own, tn)
    g_b_up = jnp.sum(g_pre_own.astype(F32), axis=0)

    g_shift2 = jnp.sum(g_normed2, axis=0)
    g_scale2 = jnp.sum(g_normed2 * x2, axis=0)
    g_mid = g_out + norm_pull(x2, r2, scale2, g_normed2)
    g_gate1 = jnp.sum(g_mid * branch, axis=0)
    g_branch = (gate1 * g_mid).astype(BF16)
    g_w_o_t = dot(g_branch, att[:, :loc], tn)
    first_sum = jnp.concatenate([g_w_up, g_w_dn_t, g_w_o_t], axis=1)
    first_sum = lax.psum_scatter(first_sum, "dp", scatter_dimension=0, tiled=True)
    g_att = jnp.concatenate(
        [dot(g_branch, wo_all[i], NT).astype(BF16) for i in range(nz)], axis=1
    )
    gq, gk, gv = attn_bwd(q, k, v, att, g_att, lse, seg_row, seg_col, lo, hi, cos, sin, nz)
    g_normed = gnormed(gq, gk, gv, w_q, w_k, w_v, wqkv)
    g_qkv = jnp.concatenate([gq[:, :loc], gk[:, :loc], gv[:, :loc]], axis=1)
    g_w_qkv = dot(normed, g_qkv, tn)
    g_shift1 = jnp.sum(g_normed, axis=0)
    g_scale1 = jnp.sum(g_normed * x1, axis=0)
    g_hidden = g_mid + norm_pull(x1, r1, scale1, g_normed)
    g_low = g_hidden.astype(BF16)
    own_low = own_cols(g_low)
    g_b_skip = jnp.sum(own_cols(g_hidden), axis=0)
    g_w_skip = jnp.concatenate([dot(frames, own_low, tn), dot(skip_in, own_low, tn)], axis=0)

    def rows_of(base):
        return lax.dynamic_slice_in_dim(wskip, base + z * loc, loc, 0).astype(BF16)

    grad_frames = dot(g_low, rows_of(0), NT)
    grad_skip = dot(g_low, rows_of(d), NT)

    g_mod = jnp.concatenate(
        [g_shift1, g_scale1, g_gate1, g_shift2, g_scale2, jnp.zeros((d,), F32)]
    )
    own_mod = lax.dynamic_slice_in_dim(g_mod, z * nm, nm, 0)
    sizes = [nm, loc, fl, d, 128]
    offs = [sum(sizes[:i]) for i in range(len(sizes) + 1)]
    vec = jnp.concatenate(
        [own_mod, g_b_skip, g_b_up, g_b_dn, jnp.broadcast_to(flow_time, (128,))]
    )[None, :]
    s_qkv, s_w_skip, vecs, gates = reduce_over_dp(
        [g_w_qkv.reshape(ndp, d // ndp, 3 * loc), g_w_skip.reshape(ndp, 2 * d // ndp, loc)],
        vec,
        g_gate2_own[None, :],
        ndp,
        nz,
        1,
    )
    vecs = vecs[:, 0]
    gate_all = gates.reshape(ndp, d)
    pad = jnp.concatenate([jnp.zeros((ndp, 5 * d), F32), gate_all], axis=1)
    mod_rows = vecs[:, :nm] + lax.dynamic_slice_in_dim(pad, z * nm, nm, 1)

    def share(i, of):
        n = sizes[i] // ndp
        cols = lax.dynamic_slice_in_dim(of, offs[i] + dp * n, n, 1)
        return jnp.sum(cols, axis=0)

    def mine(v):
        n = v.shape[1] // ndp
        return jnp.sum(lax.dynamic_slice_in_dim(v, dp * n, n, 1), axis=0)

    s_b_mod = mine(mod_rows)
    embeds = time_embed(vecs[:, offs[4]], d)
    rows = d // ndp
    s_w_mod = dot(lax.dynamic_slice_in_dim(embeds, dp * rows, rows, 1), mod_rows.astype(BF16), tn)
    s_up = first_sum[:, :fl]
    s_dn = first_sum[:, fl : 2 * fl].T
    s_o = first_sum[:, 2 * fl :].T
    return (
        output,
        grad_frames,
        grad_skip,
        s_w_skip,
        share(1, vecs),
        s_w_mod,
        s_b_mod,
        s_qkv[:, :loc],
        s_qkv[:, loc : 2 * loc],
        s_qkv[:, 2 * loc :],
        s_o,
        s_up,
        share(2, vecs),
        s_dn,
        share(3, vecs),
    )


def solution(mesh):
    in_specs = (
        P("dp", None),
        P("dp", None),
        P("dp"),
        P("dp", None),
        P(None, "tensor"),
        P("tensor"),
        P(None, "tensor"),
        P("tensor"),
        P(None, "tensor"),
        P(None, "tensor"),
        P(None, "tensor"),
        P("tensor", None),
        P(None, "tensor"),
        P("tensor"),
        P("tensor", None),
        P(),
        P("dp", None),
    )
    out_specs = (
        P("dp", "tensor"),
        P("dp", "tensor"),
        P("dp", "tensor"),
        P("dp", "tensor"),
        P(("tensor", "dp")),
        P("dp", "tensor"),
        P(("tensor", "dp")),
        P("dp", "tensor"),
        P("dp", "tensor"),
        P("dp", "tensor"),
        P("tensor", "dp"),
        P("dp", "tensor"),
        P(("tensor", "dp")),
        P("tensor", "dp"),
        P("dp"),
    )
    return jax.shard_map(
        functools.partial(per_device, mesh.shape["dp"], mesh.shape["tensor"]),
        mesh=mesh,
        in_specs=in_specs,
        out_specs=out_specs,
        check_vma=False,
    )
```

time: 1390 us -> 782 us (0.56)
  waiting for transfers between devices: 1100 us -> 0.02 us
  Pallas kernels: 0 us -> 490 us
  blocking collectives: 40.5 us -> 0 us
  matrix products: 101 us -> 135 us
  other arithmetic: 53.8 us -> 78.1 us
    psum x3 -> x0, waiting for transfers between devices: 562 us -> none  [the longest x1 262 us: per_device(): ffn = lax.psum(ffn_term, 'tensor') + b_down]
    pallas_call x0 -> x6, Pallas kernels: none -> 490 us  [the longest x1 224 us: gather(): pl.pallas_call(functools.partial(gather_kernel, chunks, nz), out_shape=ou...]
    reduce_scatter x10 -> x1, waiting for transfers between devices: 480 us -> 0.01 us  [per_device(): lax.psum_scatter(first_sum, 'dp', scatter_dimension=0, tiled=True)]
    all_gather x1 -> x0, waiting for transfers between devices: 58.8 us -> none  [per_device(): lax.all_gather(skip_part, 'tensor', axis=1, tiled=True)]
    dot_general x36 -> x33, matrix products: 101 us -> 135 us  [dot(): lax.dot_general(a, b, dims, precision=precision, preferred_element_type=F32)]
    unnamed x1 -> x0, blocking collectives: 24.1 us -> none
    another operation x6 -> x5, other arithmetic: 1.74 us -> 25 us
    dynamic_update_slice x4 -> x0, local copies, waits for them, and re-layouts: 21.9 us -> none  [attention_per_row(): lax.scan(step, (zeros, zeros), jnp.arange(count, dtype=jnp.int32))]
  transfers between devices with their start and end apart: 14 -> 1, of which waited for: 13 -> 0; matrix products, arithmetic and copies ran while one was open for 5% -> 8% of each run, Pallas kernels for 0% -> 21%
where the time goes in v1:
time: 782 us; the launch traced here: 779 us
  Pallas kernels  490 us (63%)
  matrix products  135 us (17%)
  other arithmetic  78.1 us (10%)
  local copies, waits for them, and re-layouts  59.9 us (8%)
  between operations  15.8 us (2%)
    pallas_call x1, Pallas kernels, gather(): pl.pallas_call(functools.partial(gather_kernel, chunks, nz), out_shape=ou...  224 us
    dot_general x33, matrix products, dot(): lax.dot_general(a, b, dims, precision=precision, preferred_element_type=F32)  135 us
    pallas_call x1, Pallas kernels, attn_bwd(): pl.pallas_call(functools.partial(attn_bwd_kernel, heads), out_shape=[jax....  112 us
    pallas_call x1, Pallas kernels, attn_fwd(): pl.pallas_call(functools.partial(attn_fwd_kernel, heads), out_shape=[jax....  92.1 us
    pallas_call x1, Pallas kernels, reduce_over_dp(): pl.pallas_call(functools.partial(reduce_kernel, ndp, nz, na), out_shape=[...  35.6 us
    another operation x4, other arithmetic  24.2 us
    unnamed x121, local copies, waits for them, and re-layouts  19.1 us
  transfers between devices with their start and end apart: 1, of which 0 were waited for; matrix products, arithmetic and copies ran while one was open for 8% of the time, Pallas kernels for 21%

profile of v1, /device:TPU:0, one launch (start us, length us, event | category | flops | bytes accessed | tf_op | source)
XLA Modules:
  0.0 778.5 jit_solution(4020469302204151078)
XLA Ops:
  7.3 2.9 convert_element_type.157.refs_5_
  10.2 1.6 dynamic-slice_convert_fusion.6.refs_0_
  15.5 1.5 dynamic-slice_convert_fusion.7.refs_2_
  17.0 2.1 dynamic-slice_convert_fusion.4
  19.9 223.6 %shard_map.280 = (f32[2048,1024]{1,0:T(8,128)}, f32[3,3,1024,256]{3,2,1,0:T(8,128)}, f32[3,256,1024]{2,1,0:T(8,128)}, f32[3,1024,1024]{2,1,0:T(8,128)}, f32[3,1024,1024]{2,1,0:T(8,128)}, /*index=5*/f32[4,1,2816]{2,1,0:T(1,128)}) custom-call(f32[256,256]{1,0:T(8,128)} %dynamic-slice_convert_fusion.6.refs_0_, f32[3,128,256]{2,1,0:T(8,128)} %maximum_convert_fusion.refs_1_, ...), custom_call_target="tpu_custom_call" | custom-call | tf_op jit(solution)/shard_map/pallas_call | solution.py:178
  245.3 6.2 convert.23
  251.6 1.4 convert.24
  253.0 1.9 subtract_convert_fusion
  254.9 3.3 stack.45
  259.6 4.7 fusion.5
  264.3 2.5 fusion.120
  266.8 2.1 copy-done.9
  271.6 13.6 %copy.43.sin_ref = f32[1024,256]{1,0:T(8,128)} copy(f32[1024,256]{0,1:T(8,128)S(1)} %bitcast.150) | data formatting | bytes 2097152 | tf_op jit(solution)/shard_map/tile | solution.py:728
  285.2 4.3 add_convert_fusion.1.x_ref
  289.5 13.8 %shard_map.281 = (bf16[1024,1024]{1,0:T(8,128)(2,1)}, bf16[1024,1024]{1,0:T(8,128)(2,1)}, bf16[1024,1024]{1,0:T(8,128)(2,1)}) custom-call(bf16[1024,1024]{1,0:T(8,128)(2,1)} %add_convert_fusion.1.x_ref, bf16[1024,256]{1,0:T(8,128)(2,1)} %wq_ref.3, bf16[1024,256]{1,0:T(8,128)(2,1)} %wk_ref.3, bf16[1024,256]{1,0:T(8,128)(2,1)} %wv_ref.3, ...), custom_call_target="tpu_custom_call" | custom-call | tf_op jit(solution)/shard_map/pallas_call | solution.py:384
  303.6 1.6 copy-done.3
  305.2 92.1 %shard_map.282 = (bf16[1024,1024]{1,0:T(8,128)(2,1)S(1)}, f32[4,8,1024]{2,1,0:T(8,128)S(1)}) custom-call(s32[4]{0:T(128)S(1)} %and_select_fusion.3.lo_ref, s32[4]{0:T(128)S(1)} %and_select_fusion.2.hi_ref, bf16[1024,1024]{1,0:T(8,128)(2,1)S(1)} %copy-done.3, bf16[1024,1024]{1,0:T(8,128)(2,1)} %get-tuple-element.38.k_ref, ...), custom_call_target="tpu_custom_call" | custom-call | tf_op jit(solution)/shard_map/pallas_call | solution.py:453
  397.4 2.7 fusion.54
  400.1 2.7 fusion.48
  402.8 2.8 fusion.50
  405.6 9.4 %fusion.116 = (f32[1024]{0:T(1024)S(1)}, f32[1024,1024]{1,0:T(8,128)S(1)}, f32[1024,1024]{1,0:T(8,128)}) fusion(f32[1024]{0:T(1024)S(1)} %bitcast.169, f32[1024,1024]{0,1:T(8,128)} %copy-done.9, bf16[3,256,1024]{2,1,0:T(8,128)(2,1)} %convert.24, bf16[1024,1024]{1,0:T(8,128)(2,1)S(1)} %get-tuple-element.40.att_ref, f32[1024,1024]{1,0:T(8,128)} %fusion.48, ...), kind=kOutput, calls=%fused_computation.244 | convolution fusion | flops 543161344 | bytes 26222592 | tf_op jit(solution)/shard_map/dot_general | solution.py:24
  418.0 4.4 fusion.123
  422.4 8.3 %convert.25 = bf16[3,1024,1024]{2,1,0:T(8,128)(2,1)} convert(f32[3,1024,1024]{2,1,0:T(8,128)} %get-tuple-element.42) | non-fusion elementwise | flops 3145728 | bytes 18874368 | tf_op jit(solution)/shard_map/convert.9
  430.7 6.0 fusion.16
  436.7 4.3 fusion.18
  441.0 4.7 fusion.19
  445.8 7.9 %convert_reduce_fusion = (f32[1024]{0:T(1024)S(1)}, bf16[1024,1024]{1,0:T(8,128)(2,1)S(1)}) fusion(f32[1024,1024]{1,0:T(8,128)} %fusion.123, f32[1024]{0:T(1024)S(1)} %bitcast.188, bf16[1024,1024]{1,0:T(8,128)(2,1)} %param.33, bf16[1024,1024]{1,0:T(8,128)(2,1)} %param.35, f32[1024]{0:T(1024)S(1)} %bitcast.174), kind=kOutput, calls=%fused_computation.5 | convolution fusion | flops 2171599872 | bytes 10498048 | tf_op jit(solution)/shard_map/dot_general | solution.py:24
  453.8 5.1 fusion.31
  458.8 4.4 fusion.124
  463.2 4.4 fusion.125
  467.6 8.3 %convert.26 = bf16[3,1024,1024]{2,1,0:T(8,128)(2,1)} convert(f32[3,1024,1024]{2,1,0:T(8,128)} %get-tuple-element.43) | non-fusion elementwise | flops 3145728 | bytes 18874368 | tf_op jit(solution)/shard_map/convert.8
  476.0 11.2 %fusion.17 = f32[1024,1024]{1,0:T(8,128)} fusion(bf16[3,1024,1024]{2,1,0:T(8,128)(2,1)} %convert.25, f32[1024,1024]{1,0:T(8,128)} %fusion.18, f32[1024]{0:T(1024)S(1)} %bitcast.184, bf16[1024,1024]{1,0:T(8,128)(2,1)} %param.35, f32[1024]{0:T(1024)S(1)} %bitcast.176, bf16[3,1024,1024]{2,1,0:T(8,128)(2,1)} %convert.26), kind=kOutput, calls=%fused_computation.60 | convolution fusion | flops 4316987392 | bytes 14688256 | tf_op jit(solution)/shard_map/dot_general | solution.py:24
  487.2 11.2 %fusion.15 = f32[1024,1024]{1,0:T(8,128)} fusion(bf16[3,1024,1024]{2,1,0:T(8,128)(2,1)} %convert.25, f32[1024,1024]{1,0:T(8,128)} %fusion.16, f32[1024]{0:T(1024)S(1)} %bitcast.186, bf16[1024,1024]{1,0:T(8,128)(2,1)} %param.35, f32[1024]{0:T(1024)S(1)} %bitcast.177, bf16[3,1024,1024]{2,1,0:T(8,128)(2,1)} %convert.26), kind=kOutput, calls=%fused_computation.58 | convolution fusion | flops 4316987392 | bytes 14688256 | tf_op jit(solution)/shard_map/dot_general | solution.py:24
  498.3 15.1 %multiply_reduce_fusion = (f32[1024]{0:T(1024)S(1)}, f32[1024]{0:T(1024)S(1)}, f32[1024]{0:T(1024)S(1)}, f32[1024]{0:T(1024)S(1)}, f32[1024,1024]{1,0:T(8,128)}) fusion(f32[1024,1024]{1,0:T(8,128)} %copy-done.11, f32[1024]{0:T(1024)S(1)} %add_rsqrt_fusion, f32[1024]{0:T(1024)S(1)} %broadcast_multiply_fusion.4, f32[1024]{0:T(1024)S(1)} %bitcast.172, ...), kind=kOutput, calls=%fused_computation.6 | convolution fusion | flops 4329566208 | bytes 31494144 | tf_op jit(solution)/shard_map/dot_general | solution.py:24
  513.4 6.2 multiply_reduce_fusion.1
  519.6 2.0 copy-done.12
  522.3 1.4 copy-done.28
  524.4 9.0 %pad_maximum_fusion = f32[1024,2304]{0,1:T(8,128)} fusion(f32[1024,256]{0,1:T(8,128)S(1)} %fusion.52, f32[1024,1024]{0,1:T(8,128)} %fusion.31, f32[1024,1024]{0,1:T(8,128)} %fusion.125), kind=kLoop, calls=%fused_computation.2 | loop fusion | flops 4718592 | bytes 18874368 | tf_op jit(solution)/shard_map/concatenate | solution.py:773
  533.5 1.6 copy-done.15
  535.0 2.4 convert_element_type.177
  537.5 3.3 convolution_convert_fusion
  544.4 1.6 pad_maximum_fusion.1.g_ref
  546.1 111.6 %shard_map.283 = (bf16[1024,1024]{1,0:T(8,128)(2,1)}, bf16[1024,1024]{1,0:T(8,128)(2,1)}, bf16[1024,1024]{1,0:T(8,128)(2,1)}) custom-call(s32[4]{0:T(128)} %copy-done.7, s32[4]{0:T(128)} %copy-done.8, bf16[1024,1024]{1,0:T(8,128)(2,1)} %get-tuple-element.37.q_ref, bf16[1024,1024]{1,0:T(8,128)(2,1)} %get-tuple-element.38.k_ref, ...), custom_call_target="tpu_custom_call" | custom-call | tf_op jit(solution)/shard_map/pallas_call | solution.py:562
  657.7 1.9 slice.154
  659.6 1.9 slice.153
  661.5 13.1 %shard_map.284 = f32[1024,1024]{1,0:T(8,128)} custom-call(bf16[1024,1024]{1,0:T(8,128)(2,1)} %get-tuple-element.45.gq_ref, bf16[1024,1024]{1,0:T(8,128)(2,1)} %get-tuple-element.46.gk_ref, bf16[1024,1024]{1,0:T(8,128)(2,1)} %get-tuple-element.47.gv_ref, bf16[1024,256]{1,0:T(8,128)(2,1)} %wq_ref.3, bf16[1024,256]{1,0:T(8,128)(2,1)} %wk_ref.3, ...), custom_call_target="tpu_custom_call" | custom-call | tf_op jit(solution)/shard_map/pallas_call | solution.py:609
  674.5 1.9 slice.152
  677.2 5.0 multiply_reduce_fusion.2
  683.1 4.6 fusion.115
  690.0 2.0 copy.50
  692.0 1.4 dynamic-slice_reduce_fusion
  694.2 3.7 fusion.117
  698.1 3.6 fusion.22
  701.7 2.8 convolution_add_fusion
  704.5 1.7 fusion.30
  706.7 1.6 fusion.29
  708.9 4.8 multiply_reduce_fusion.9
  713.7 35.6 %shard_map.285 = (f32[128,768]{1,0:T(8,128)}, f32[256,256]{1,0:T(8,128)}, f32[8,1,3968]{2,1,0:T(1,128)}, f32[8,4,1,256]{3,2,1,0:T(1,128)}) custom-call(f32[8,128,768]{2,1,0:T(8,128)} %bitcast.152, f32[8,256,256]{2,1,0:T(8,128)} %bitcast.149, f32[1,3968]{1,0:T(1,128)} %broadcast_in_dim.66.refs_2_, f32[1,256]{1,0:T(1,128)} %bitcast.193), custom_call_target="tpu_custom_call" | custom-call | tf_op jit(solution)/shard_map/pallas_call | solution.py:331
  754.6 1.8 fusion.118
  757.6 3.7 fusion.38
  761.3 3.6 fusion.39
  764.9 2.2 slice_bitcast_fusion.9
  767.1 2.0 copy.51
  769.2 1.6 slice_bitcast_fusion.19
  (186 shorter events, 30.9 us)
Async XLA Ops:
  7.2 5.4 copy-start
  7.2 5.9 copy-start.45
  7.2 6.0 copy-start.46
  7.2 6.0 copy-start.47
  7.2 757.7 %reduce-scatter.2.cloned.1.call-start = ((), (), s32[]{:S(2)}) async-start(), calls=%async_computation.1 | async-start | bytes 10616832 | tf_op jit(solution)/shard_map/reduce_scatter | solution.py:774
  13.1 231.2 %copy-start.42 = (s32[1,1024]{1,0:T(1,128)S(1)}, s32[1,1024]{1,0:T(1,128)}, u32[]{:S(2)}) copy-start(s32[1,1024]{1,0:T(1,128)} %param.22) | copy-start | bytes 12292
  245.3 39.9 %copy-start.38 = (f32[1,1024]{1,0:T(1,128)}, f32[1,1024]{1,0:T(1,128)S(1)}, u32[]{:S(2)}) copy-start(f32[1,1024]{1,0:T(1,128)S(1)} %get-tuple-element.118) | copy-start | bytes 12292
  245.3 6.2 copy-start.22
  258.9 44.7 %copy-start.7 = (s32[4]{0:T(128)}, s32[4]{0:T(128)S(1)}, u32[]{:S(2)}) copy-start(s32[4]{0:T(128)S(1)} %and_select_fusion.3.lo_ref) | copy-start | bytes 52
  259.6 44.0 %copy-start.8 = (s32[4]{0:T(128)}, s32[4]{0:T(128)S(1)}, u32[]{:S(2)}) copy-start(s32[4]{0:T(128)S(1)} %and_select_fusion.2.hi_ref) | copy-start | bytes 52
  259.6 4.7 copy-start.21
  259.6 4.7 copy-start.26
  266.8 2.1 copy-start.9
  266.8 18.4 %copy-start.36 = (f32[1024]{0:T(1024)}, f32[1024]{0:T(1024)S(1)}, u32[]{:S(2)}) copy-start(f32[1024]{0:T(1024)S(1)} %broadcast_multiply_fusion.5) | copy-start | bytes 12292
  269.5 20.1 %copy-start.40 = (f32[1024]{0:T(1024)}, f32[1024]{0:T(1024)S(1)}, u32[]{:S(2)}) copy-start(f32[1024]{0:T(1024)S(1)} %add_rsqrt_fusion.1) | copy-start | bytes 12292
  303.3 94.0 %copy-start.30 = (bf16[256,1024]{1,0:T(8,128)(2,1)S(1)}, bf16[256,1024]{1,0:T(8,128)(2,1)}, u32[]{:S(2)}) copy-start(bf16[256,1024]{1,0:T(8,128)(2,1)} %param.30) | copy-start | bytes 1572868
  303.3 96.7 %copy-start.5 = (s32[1,8,1024]{2,1,0:T(8,128)}, s32[1,8,1024]{2,1,0:T(8,128)S(1)}, u32[]{:S(2)}) copy-start(s32[1,8,1024]{2,1,0:T(8,128)S(1)} %broadcast_in_dim.61.segq_ref) | copy-start | bytes 98308
  303.6 1.6 copy-start.3
  305.2 94.9 %copy-start.4 = (s32[1024,128]{1,0:T(8,128)}, s32[1024,128]{1,0:T(8,128)S(1)}, u32[]{:S(2)}) copy-start(s32[1024,128]{1,0:T(8,128)S(1)} %broadcast_in_dim.62.segk_ref) | copy-start | bytes 1572868
  397.3 2.8 copy-start.6
  397.3 125.0 %copy-start.2 = (bf16[1024,1024]{1,0:T(8,128)(2,1)}, bf16[1024,1024]{1,0:T(8,128)(2,1)S(1)}, u32[]{:S(2)}) copy-start(bf16[1024,1024]{1,0:T(8,128)(2,1)S(1)} %get-tuple-element.40.att_ref) | copy-start | bytes 6291460
  397.4 2.7 copy-start.17
  414.9 2.0 copy-start.11
  415.5 2.5 copy-start.43
  418.0 23.0 %copy-start.23 = (bf16[1024,1024]{1,0:T(8,128)(2,1)}, bf16[1024,1024]{1,0:T(8,128)(2,1)S(1)}, u32[]{:S(2)}) copy-start(bf16[1024,1024]{1,0:T(8,128)(2,1)S(1)} %add_convert_fusion) | copy-start | bytes 6291460
  430.7 6.0 copy-start.19
  445.8 8.0 %copy-start.14 = (bf16[1024,1024]{1,0:T(8,128)(2,1)S(1)}, bf16[1024,1024]{1,0:T(8,128)(2,1)}, u32[]{:S(2)}) copy-start(bf16[1024,1024]{1,0:T(8,128)(2,1)} %param.35) | copy-start | bytes 6291460
  445.8 8.0 %copy-start.51 = (f32[1024,1024]{1,0:T(8,128)S(1)}, f32[1024,1024]{1,0:T(8,128)}, u32[]{:S(2)}) copy-start(f32[1024,1024]{1,0:T(8,128)} %fusion.123) | copy-start | bytes 12582916
  453.7 5.1 copy-start.44
  458.8 4.4 copy-start.24
  519.6 2.0 copy-start.12
  522.3 1.4 copy-start.28
  533.4 1.6 copy-start.15
  537.5 3.3 copy-start.18
  537.5 4.3 copy-start.29
  542.6 1.1 copy-start.31
  661.5 15.7 %copy-start.37 = (f32[1024]{0:T(1024)S(1)}, f32[1024]{0:T(1024)}, u32[]{:S(2)}) copy-start(f32[1024]{0:T(1024)} %copy-done.36) | copy-start | bytes 12292
  661.5 15.7 %copy-start.39 = (f32[1,1024]{1,0:T(1,128)S(1)}, f32[1,1024]{1,0:T(1,128)}, u32[]{:S(2)}) copy-start(f32[1,1024]{1,0:T(1,128)} %copy-done.38) | copy-start | bytes 12292
  661.5 15.7 %copy-start.41 = (f32[1024]{0:T(1024)S(1)}, f32[1024]{0:T(1024)}, u32[]{:S(2)}) copy-start(f32[1024]{0:T(1024)} %copy-done.40) | copy-start | bytes 12292
  677.1 5.0 copy-start.10
  677.2 5.9 copy-start.13
  683.1 4.6 copy-start.25
  683.1 6.0 copy-start.27
  687.7 1.4 copy-start.20
  694.2 3.8 copy-start.16
  694.2 3.8 copy-start.32
  694.2 3.8 copy-start.33
  694.2 3.8 copy-start.34
  698.1 3.6 copy-start.52
  701.7 2.8 copy-start.50
  704.5 2.2 copy-start.49
  706.7 2.2 copy-start.48
  757.5 13.9 %copy-start.1 = (bf16[1024,1536]{1,0:T(8,128)(2,1)S(1)}, bf16[1024,1536]{1,0:T(8,128)(2,1)}, u32[]{:S(2)}) copy-start(bf16[1024,1536]{1,0:T(8,128)(2,1)} %param.25) | copy-start | bytes 9437188
  761.3 9.5 %copy-start.35 = (f32[256,256]{1,0:T(8,128)S(1)}, f32[256,256]{1,0:T(8,128)}, u32[]{:S(2)}) copy-start(f32[256,256]{1,0:T(8,128)} %get-tuple-element.161) | copy-start | bytes 786436
Sparse Core Ops, SparseCore 0:
  533.6 73.2 reduce-scatter.1

commit v2 on v1

v2 whole, which is shorter than its diff:
```python
import functools
import math

import jax
import jax.numpy as jnp
from jax import lax
from jax.experimental import pallas as pl
from jax.experimental.pallas import tpu as pltpu
from jax.sharding import PartitionSpec as P

HEAD_DIM = 64
EPS = 1e-06
F32 = jnp.float32
BF16 = jnp.bfloat16
MESH = pl.DeviceIdType.MESH
ANY = pl.BlockSpec(memory_space=pl.ANY)
VMEM = pl.BlockSpec(memory_space=pltpu.VMEM)
GROUP = 8
NT = (((1,), (1,)), ((), ()))
NN = (((1,), (0,)), ((), ()))


def dot(a, b, dims=NN, precision=None):
    return lax.dot_general(a, b, dims, precision=precision, preferred_element_type=F32)


def remote(src, dst, send, recv, device):
    return pltpu.make_async_remote_copy(
        src_ref=src,
        dst_ref=dst,
        send_sem=send,
        recv_sem=recv,
        device_id=device,
        device_id_type=MESH,
    )


class Spread:
    def __init__(self, nz, n, src, view, sems, lags):
        self.nz, self.n, self.src, self.view, self.lags = nz, n, src, view, lags
        self.zs, self.zr, self.ps, self.pr = sems
        dp = lax.axis_index("dp")
        z = lax.axis_index("tensor")
        self.z = z
        p = lax.rem(dp, GROUP)
        self.p = p
        core = lax.rem(dp, 2)
        ds_ = 1 - 2 * core
        dx = 2 - 4 * lax.rem(dp // 2, 2)
        dy = 4 - 8 * lax.rem(dp // 4, 2)
        d1 = dy + core * (dx - dy)
        d2 = dx + core * (dy - dx)
        self.near = {1: (dp + d1, z), 2: (dp + d2, z), 3: (dp + ds_, z)}
        self.far = {k: (dp, lax.rem(z + nz - k, nz)) for k in range(1, nz)}
        self.stages = {
            1: ([p], d1, 0),
            2: ([p, p + d1], d2, 1),
            3: ([p, p + d1, p + d2, p + d1 + d2], ds_, 3),
        }
        self.t = 0
        self.ready = -1

    def barrier(self):
        bar = pltpu.get_barrier_semaphore()
        devices = list(self.near.values()) + list(self.far.values())
        for device in devices:
            pl.semaphore_signal(bar, inc=1, device_id=device, device_id_type=MESH)
        pl.semaphore_wait(bar, len(devices))

    def _far(self, i, k, zz):
        return remote(
            self.src(i),
            self.view(i, k, self.p, zz),
            self.zs.at[i, k - 1],
            self.zr.at[i, k - 1],
            self.far[k],
        )

    def _near(self, i, stage, inward):
        qs, shift, base = self.stages[stage]
        kk = self.nz - 1
        out = []
        for j, q in enumerate(qs):
            if inward:
                q = q + shift
            for k in range(1, self.nz):
                ref = self.view(i, k, q, lax.rem(self.z + k, self.nz))
                s = (base + j) * kk + k - 1
                out.append(
                    functools.partial(
                        remote, ref, ref, self.ps.at[i, s], self.pr.at[i, s], self.near[stage]
                    )
                )
        return out

    def tick(self):
        t, n = self.t, self.n
        l1, l2, l3, l4 = self.lags
        if t < n:
            for k in range(1, self.nz):
                self._far(t, k, self.z).start()
        if 0 <= t - l4 < n:
            for c in self._near(t - l4, 3, True):
                c().wait_recv()
            self.ready = t - l4
        for stage, lag in ((3, l3), (2, l2)):
            if 0 <= t - lag < n:
                for c in self._near(t - lag, stage - 1, True):
                    c().wait_recv()
                for c in self._near(t - lag, stage, False):
                    c().start()
        if 0 <= t - l1 < n:
            for k in range(1, self.nz):
                self._far(t - l1, k, lax.rem(self.z + k, self.nz)).wait_recv()
            for c in self._near(t - l1, 1, False):
                c().start()
        self.t += 1

    def until(self, i):
        while self.ready < i:
            self.tick()

    def drain(self):
        for i in range(self.n):
            for k in range(1, self.nz):
                self._far(i, k, self.z).wait_send()
            for stage in (1, 2, 3):
                for c in self._near(i, stage, False):
                    c().wait_send()


def spread_sems(nz, n):
    dma = pltpu.SemaphoreType.DMA
    kk = nz - 1
    return [dma((n, kk)), dma((n, kk)), dma((n, 7 * kk)), dma((n, 7 * kk))]


def layer_norm(v):
    centred = v - jnp.mean(v, axis=-1, keepdims=True)
    r = lax.rsqrt(jnp.mean(centred * centred, axis=-1, keepdims=True) + EPS)
    return centred * r, r


TB = 512
LB = 128


def first_kernel(nz, chunks, *refs):
    (x_ref, y_ref, wskip_ref, wq_ref, wk_ref, wv_ref, wo_ref, vec_ref, cos_ref, sin_ref) = refs[:10]
    (hid_ref, norm_ref, q_ref, k_ref, v_ref, lskip, lqkv, lo_, small_ref) = refs[10:19]
    (pskip, pqkv, po, fskip, sskip, sqkv, wb, loc_sem, st_sem, vs, vr) = refs[19:30]
    sems = refs[30:34]
    t, d = x_ref.shape
    loc = wq_ref.shape[1]
    own = {"skip": wskip_ref, "qkv": (wq_ref, wk_ref, wv_ref), "o": wo_ref}
    rs, rq, ro = pskip.shape[0], pqkv.shape[1], po.shape[0]

    def src(i):
        name, a, off, r = chunks[i]
        if name == "skip":
            return pskip.at[pl.ds(off, r)]
        if name == "qkv":
            return pqkv.at[a, pl.ds(off, r)]
        return po.at[pl.ds(off, r)]

    def view(i, k, q, zz):
        name, a, off, r = chunks[i]
        if name == "skip":
            return lskip.at[pl.ds(q * rs + off, r), pl.ds(pl.multiple_of(zz * loc, loc), loc)]
        if name == "qkv":
            return lqkv.at[k - 1, a, pl.ds(q * rq + off, r)]
        return lo_.at[k - 1, pl.ds(q * ro + off, r)]

    net = Spread(nz, len(chunks), src, view, sems, (1, 2, 3, 4))
    z, p = net.z, net.p
    pskip[...] = wskip_ref[pl.ds(pl.multiple_of(p * rs, rs), rs), :].astype(F32)
    net.barrier()

    def vec(k, zz):
        return remote(vec_ref, small_ref.at[zz], vs.at[k - 1], vr.at[k - 1], net.far[k])

    for k in range(1, nz):
        vec(k, z).start()
    net.tick()
    for a, w in enumerate((wq_ref, wk_ref, wv_ref)):
        pqkv[a] = w[pl.ds(pl.multiple_of(p * rq, rq), rq), :].astype(F32)
    po[...] = wo_ref[pl.ds(pl.multiple_of(p * ro, ro), ro), :].astype(F32)
    net.tick()
    small_ref[z] = vec_ref[...]
    fskip[...] = wskip_ref[...].astype(F32)

    def cols(zz):
        return pl.ds(pl.multiple_of(zz * loc, loc), loc)

    keep = lambda: pltpu.make_async_copy(fskip, lskip.at[:, cols(z)], loc_sem.at[0])
    keep().start()
    for k in range(1, nz):
        vec(k, lax.rem(z + k, nz)).wait_recv()
    nm = 6 * d // nz

    def flat(lo, hi):
        parts = []
        while lo < hi:
            zz = lo // nm
            end = min(hi, (zz + 1) * nm)
            parts.append(small_ref[zz, :, lo - zz * nm : end - zz * nm])
            lo = end
        return jnp.concatenate(parts, axis=1)

    def hidden_cols(w, zz):
        bias = small_ref[zz, :, nm : nm + loc]

        @pl.loop(0, t // TB)
        def _(b):
            rows = pl.ds(pl.multiple_of(b * TB, TB), TB)
            acc = dot(x_ref[rows, :], w[:d, :]) + dot(y_ref[rows, :], w[d:, :])
            hid_ref[rows, cols(zz)] = acc + bias

    hidden_cols(wskip_ref, z)
    nskip = sum(c[0] == "skip" for c in chunks)
    net.until(nskip - 1)
    stage = lambda k: pltpu.make_async_copy(
        lskip.at[:, cols(lax.rem(z + k, nz))], sskip.at[k - 1], st_sem.at[k - 1]
    )
    for k in range(1, nz):
        stage(k).start()
    for k in range(1, nz):
        stage(k).wait()
        wb[...] = sskip[k - 1].astype(BF16)
        hidden_cols(wb, lax.rem(z + k, nz))
        net.tick()
    shift1, scale1 = flat(0, d), flat(d, 2 * d)

    @pl.loop(0, t // LB)
    def _(b):
        rows = pl.ds(pl.multiple_of(b * LB, LB), LB)
        xn, _ = layer_norm(hid_ref[rows, :])
        norm_ref[rows, :] = (xn * (1.0 + scale1) + shift1).astype(BF16)

    net.tick()

    def project(a, k, w):
        out = (q_ref, k_ref, v_ref)[a]

        @pl.loop(0, t // TB)
        def _(b):
            rows = pl.ds(pl.multiple_of(b * TB, TB), TB)
            u = dot(norm_ref[rows, :], w[...])
            if a < 2:
                u = u * cos_ref[rows, :] + swap_halves(u) * sin_ref[rows, :]
            if a == 0:
                u = u.astype(BF16).astype(F32) * (HEAD_DIM**-0.5)
            out[rows, k * loc : (k + 1) * loc] = u.astype(BF16)

    for a in range(3):
        project(a, 0, (wq_ref, wk_ref, wv_ref)[a])
    nq = sum(c[0] == "qkv" for c in chunks) // 3
    bring = lambda a: pltpu.make_async_copy(lqkv.at[:, a], sqkv.at[a % 2], st_sem.at[a % 2])
    for a in range(3):
        net.until(nskip + nq * (a + 1) - 1)
        bring(a).start()
        bring(a).wait()
        for k in range(1, nz):
            wb[:d, :] = sqkv[a % 2, k - 1].astype(BF16)
            project(a, k, wb.at[:d, :])
            if a < 2:
                net.tick()
    net.until(len(chunks) - 1)
    net.drain()
    for k in range(1, nz):
        vec(k, z).wait_send()
    keep().wait()


def first(x, y, wskip, wq, wk, wv, wo, vec, cos, sin, nz):
    t, d = x.shape
    loc = wq.shape[1]
    chunks = []
    rs, rq, ro = 2 * d // GROUP, d // GROUP, loc // GROUP
    for j in range(4):
        chunks.append(("skip", 0, j * rs // 4, rs // 4))
    for a in range(3):
        for j in range(2):
            chunks.append(("qkv", a, j * rq // 2, rq // 2))
    for j in range(2):
        chunks.append(("o", 0, j * ro // 2, ro // 2))
    sd = jax.ShapeDtypeStruct
    kk = nz - 1
    dma = pltpu.SemaphoreType.DMA
    outs = [
        sd((t, d), F32),
        sd((t, d), BF16),
        sd((t, nz * loc), BF16),
        sd((t, nz * loc), BF16),
        sd((t, nz * loc), BF16),
        sd((2 * d, nz * loc), F32),
        sd((kk, 3, d, loc), F32),
        sd((kk, loc, d), F32),
        sd((nz,) + vec.shape, F32),
    ]
    scratch = [
        pltpu.VMEM((rs, loc), F32),
        pltpu.VMEM((3, rq, loc), F32),
        pltpu.VMEM((ro, d), F32),
        pltpu.VMEM((2 * d, loc), F32),
        pltpu.VMEM((kk, 2 * d, loc), F32),
        pltpu.VMEM((2, kk, d, loc), F32),
        pltpu.VMEM((2 * d, loc), BF16),
        dma((1,)),
        dma((max(kk, 2),)),
        dma((kk,)),
        dma((kk,)),
    ] + spread_sems(nz, len(chunks))
    return pl.pallas_call(
        functools.partial(first_kernel, nz, chunks),
        out_shape=outs,
        in_specs=[VMEM] * 10,
        out_specs=[VMEM] * 5 + [ANY] * 3 + [VMEM],
        scratch_shapes=scratch,
        compiler_params=pltpu.CompilerParams(
            collective_id=0, has_side_effects=True, vmem_limit_bytes=60 << 20
        ),
    )(x, y, wskip, wq, wk, wv, wo, vec, cos, sin)


def gelu_parts(v):
    c = math.sqrt(2.0 / math.pi)
    v2 = v * v
    th = jnp.tanh(c * v * (1.0 + 0.044715 * v2))
    half = 0.5 * (1.0 + th)
    act = v * half
    slope = half + (0.5 * c) * v * (1.0 - th * th) * (1.0 + 3.0 * 0.044715 * v2)
    return act, slope


TN = (((0,), (0,)), ((), ()))


def second_kernel(nz, n, r, per, *refs):
    (att_ref, hid_ref, go_ref, woo_ref, wo_ref, up_ref, dn_ref, mod_ref, bup_ref, bupr_ref, bdn_ref) = refs[:11]
    (out_ref, gm_ref, gb_ref, ga_ref, gw_ref, sums_ref, gbu_ref, gg2_ref, land) = refs[11:20]
    (pc, wob, br_ref, n2_ref, gf_ref, stg, ub, db, act_s, gp_s, gws, st_sem, gw_sem) = refs[20:33]
    sems = refs[33:37]
    t, d = hid_ref.shape
    loc = woo_ref.shape[0]
    fl = up_ref.shape[1]
    kk = nz - 1
    pr = fl // GROUP
    net = Spread(
        nz,
        n,
        lambda i: pc.at[:, pl.ds(i * r, r)],
        lambda i, k, q, zz: land.at[i, :, k - 1, q],
        sems,
        (1, 2, 3, 4),
    )
    z, p = net.z, net.p
    own = pl.ds(pl.multiple_of(z * loc, loc), loc)
    pc[0] = up_ref[:, pl.ds(pl.multiple_of(p * pr, pr), pr)].astype(F32).T
    pc[1] = dn_ref[pl.ds(pl.multiple_of(p * pr, pr), pr), :].astype(F32)
    net.barrier()
    net.tick()
    row = lambda i: mod_ref[i : i + 1, :]
    gate1, shift2, scale2, gate2 = row(2), row(3), row(4), row(5)
    for k in range(1, nz):
        wob[k] = wo_ref[k - 1].astype(BF16)
    wob[0] = woo_ref[...]
    net.tick()

    @pl.loop(0, t // TB)
    def _(b):
        rows = pl.ds(pl.multiple_of(b * TB, TB), TB)
        br_ref[rows, :] = dot(att_ref[rows, :], wob[...].reshape(nz * loc, d))

    net.tick()
    sums_ref[...] = jnp.zeros_like(sums_ref)

    @pl.loop(0, t // LB)
    def _(b):
        rows = pl.ds(pl.multiple_of(b * LB, LB), LB)
        x2, _ = layer_norm(hid_ref[rows, :] + gate1 * br_ref[rows, :])
        n2_ref[rows, :] = (x2 * (1.0 + scale2) + shift2).astype(BF16)
        go = go_ref[rows, :].astype(F32)
        sums_ref[3:4, :] += jnp.sum(go, axis=0, keepdims=True)
        gf_ref[rows, :] = (gate2 * go).astype(BF16)

    def units(first_time, rows, pre, dnv, uv_g):
        act, slope = gelu_parts(pre)
        actl = act.astype(BF16)
        ffn = dot(actl, dnv[:, own])
        g_pre = (dot(gf_ref[rows, :], dnv[...], NT) * slope).astype(BF16)
        gn = uv_g(g_pre)
        if first_time:
            out_ref[rows, :] = ffn
            gm_ref[rows, :] = gn
        else:
            out_ref[rows, :] += ffn
            gm_ref[rows, :] += gn
        return actl, g_pre

    sub = fl // 4
    gwc = lambda j, s: pltpu.make_async_copy(
        gws.at[s], gw_ref.at[pl.ds(s * fl + j * sub, sub)], gw_sem.at[s]
    )
    for j in range(4):
        net.tick()
        cs = slice(j * sub, (j + 1) * sub)

        @pl.loop(0, t // TB)
        def _(b):
            rows = pl.ds(pl.multiple_of(b * TB, TB), TB)
            pre = dot(n2_ref[rows, :], up_ref[:, cs]) + bup_ref[:, cs]
            a, g = units(
                j == 0, rows, pre, dn_ref.at[cs, :], lambda gp: dot(gp, up_ref[:, cs], NT)
            )
            act_s[rows, :] = a
            gp_s[rows, :] = g

        if j > 0:
            for s in range(2):
                gwc(j - 1, s).wait()
        gbu_ref[:, cs] = jnp.sum(gp_s[...].astype(F32), axis=0, keepdims=True)
        gws[0] = dot(gp_s[...], n2_ref[...], TN)
        gws[1] = dot(act_s[...], gf_ref[...], TN)
        for s in range(2):
            gwc(j, s).start()
    for s in range(2):
        gwc(3, s).wait()

    nu = per * kk * GROUP * r
    steps = n // per

    def fetch(m):
        return pltpu.make_async_copy(
            land.at[pl.ds(m * per, per)], stg.at[m % 2], st_sem.at[m % 2]
        )

    for m in range(steps):
        net.until(m * per + per - 1)
        fetch(m).start()
        if m + 1 < steps:
            net.tick()
        fetch(m).wait()
        for c in range(per):
            w = nu // per
            ub[c * w : (c + 1) * w, :] = stg[m % 2, c, 0].reshape(w, d).astype(BF16)
            db[c * w : (c + 1) * w, :] = stg[m % 2, c, 1].reshape(w, d).astype(BF16)

        @pl.loop(0, t // TB)
        def _(b):
            rows = pl.ds(pl.multiple_of(b * TB, TB), TB)
            pre = dot(n2_ref[rows, :], ub[...], NT) + bupr_ref[m]
            units(False, rows, pre, db, lambda gp: dot(gp, ub[...]))

    net.drain()
    bdn = bdn_ref[:, own]
    gate2_own = mod_ref[5:6, own]
    gate1_own = mod_ref[2:3, own]

    @pl.loop(0, t // LB)
    def _(b):
        rows = pl.ds(pl.multiple_of(b * LB, LB), LB)
        ffn = out_ref[rows, :] + bdn
        go_own = go_ref[rows, own].astype(F32)
        gg2 = jnp.sum(go_own * ffn, axis=0, keepdims=True)

        @pl.when(b == 0)
        def _():
            gg2_ref[...] = gg2

        @pl.when(b > 0)
        def _():
            gg2_ref[...] += gg2

        out_ref[rows, :] = hid_ref[rows, own] + gate1_own * br_ref[rows, own] + gate2_own * ffn
        br = br_ref[rows, :]
        x2, r2 = layer_norm(hid_ref[rows, :] + gate1 * br)
        gn = gm_ref[rows, :]
        sums_ref[0:1, :] += jnp.sum(gn, axis=0, keepdims=True)
        sums_ref[1:2, :] += jnp.sum(gn * x2, axis=0, keepdims=True)
        gp = gn * (1.0 + scale2)
        gm = go_ref[rows, :].astype(F32) + r2 * (
            gp
            - jnp.mean(gp, axis=-1, keepdims=True)
            - x2 * jnp.mean(gp * x2, axis=-1, keepdims=True)
        )
        gm_ref[rows, :] = gm
        sums_ref[2:3, :] += jnp.sum(gm * br, axis=0, keepdims=True)
        gb_ref[rows, :] = (gate1 * gm).astype(BF16)

    @pl.loop(0, t // TB)
    def _(b):
        rows = pl.ds(pl.multiple_of(b * TB, TB), TB)
        ga_ref[rows, :] = dot(gb_ref[rows, :], wob[...].reshape(nz * loc, d), NT).astype(BF16)

    gws[0, :loc, :] = dot(att_ref[:, :loc], gb_ref[...], TN)
    last = pltpu.make_async_copy(gws.at[0, :loc], gw_ref.at[pl.ds(2 * fl, loc)], gw_sem.at[0])
    last.start()
    last.wait()


def second(att, hid, go, wo_own, wo, up, dn, mod, bup_own, bup_rest, bdn, nz, r=8, per=2):
    t, d = hid.shape
    loc = wo_own.shape[0]
    fl = up.shape[1]
    kk = nz - 1
    n = fl // GROUP // r
    nu = per * kk * GROUP * r
    sd = jax.ShapeDtypeStruct
    dma = pltpu.SemaphoreType.DMA
    outs = [
        sd((t, loc), F32),
        sd((t, d), F32),
        sd((t, d), BF16),
        sd((t, nz * loc), BF16),
        sd((2 * fl + loc, d), F32),
        sd((8, d), F32),
        sd((1, fl), F32),
        sd((1, loc), F32),
        sd((n, 2, kk, GROUP, r, d), F32),
    ]
    scratch = [
        pltpu.VMEM((2, fl // GROUP, d), F32),
        pltpu.VMEM((nz, loc, d), BF16),
        pltpu.VMEM((t, d), F32),
        pltpu.VMEM((t, d), BF16),
        pltpu.VMEM((t, d), BF16),
        pltpu.VMEM((2, per, 2, kk, GROUP, r, d), F32),
        pltpu.VMEM((nu, d), BF16),
        pltpu.VMEM((nu, d), BF16),
        pltpu.VMEM((t, fl // 4), BF16),
        pltpu.VMEM((t, fl // 4), BF16),
        pltpu.VMEM((2, max(fl // 4, loc), d), F32),
        dma((2,)),
        dma((2,)),
    ] + spread_sems(nz, n)
    b = bup_rest.reshape(kk, GROUP, n // per, per, r).transpose(2, 3, 0, 1, 4)
    b = b.reshape(n // per, 1, nu)
    return pl.pallas_call(
        functools.partial(second_kernel, nz, n, r, per),
        out_shape=outs,
        in_specs=[VMEM] * 11,
        out_specs=[VMEM] * 4 + [ANY] + [VMEM] * 3 + [ANY],
        scratch_shapes=scratch,
        compiler_params=pltpu.CompilerParams(
            collective_id=2, has_side_effects=True, vmem_limit_bytes=62 << 20
        ),
    )(att, hid, go, wo_own, wo, up, dn, mod, bup_own, b, bdn)


def reduce_kernel(ndp, nz, na, *refs):
    bits = ndp.bit_length() - 1
    ins = refs[:na]
    small, part = refs[na : na + 2]
    outs = refs[na + 2 : 2 * na + 2]
    all_small, all_part = refs[2 * na + 2 : 2 * na + 4]
    rest = refs[2 * na + 4 :]
    recv0, lev0 = rest[:na], rest[na : 2 * na]
    half_refs = rest[2 * na : -8]
    gz, s_send, s_recv, q_send, q_recv, z_send, z_recv, l_sem = rest[-8:]
    dp = lax.axis_index("dp")
    z = lax.axis_index("tensor")
    mine = [lax.rem(dp // (1 << b), 2) for b in range(bits)]
    partner = [(dp + (1 << b) * (1 - 2 * mine[b]), z) for b in range(bits)]
    bar = pltpu.get_barrier_semaphore()

    def others(j):
        return lax.rem(dp + j, ndp)

    for j in range(1, ndp):
        pl.semaphore_signal(bar, inc=1, device_id=(others(j), z), device_id_type=MESH)
    for k in range(1, nz):
        pl.semaphore_signal(bar, inc=1, device_id=(dp, lax.rem(z + k, nz)), device_id_type=MESH)
    pl.semaphore_wait(bar, ndp - 1 + nz - 1)

    def gzc(k, zz):
        return remote(part, gz.at[zz], z_send.at[k - 1], z_recv.at[k - 1], (dp, lax.rem(z + nz - k, nz)))

    for k in range(1, nz):
        gzc(k, z).start()

    def first(a, i):
        s = 2 * i + 1 - mine[0]
        return remote(ins[a].at[s], recv0[a].at[i], s_send.at[a, i], s_recv.at[a, i], partner[0])

    for a in range(na):
        for i in range(ndp // 2):
            first(a, i).start()
    gz[z] = part[...]

    def sml(j, row):
        return remote(small, all_small.at[row], q_send.at[0, j - 1], q_recv.at[0, j - 1], (others(j), z))

    def prt(j, row):
        return remote(gz, all_part.at[row], q_send.at[1, j - 1], q_recv.at[1, j - 1], (others(j), z))

    own = [
        lambda: pltpu.make_async_copy(small, all_small.at[dp], l_sem.at[0]),
        lambda: pltpu.make_async_copy(gz, all_part.at[dp], l_sem.at[1]),
    ]
    for j in range(1, ndp):
        sml(j, dp).start()
    own[0]().start()
    for k in range(1, nz):
        gzc(k, lax.rem(z + k, nz)).wait_recv()
    for j in range(1, ndp):
        prt(j, dp).start()
    own[1]().start()
    for a in range(na):
        for i in range(ndp // 2):
            first(a, i).wait_recv()
            lev0[a][i] = ins[a][2 * i + mine[0]] + recv0[a][i]
    orders = [list(range(1, bits)), list(range(bits - 1, 0, -1))]
    state = {}
    pos = 0
    for a in range(na):
        for h in range(2):
            cw = ins[a].shape[2] // 2
            state[a, h] = (lev0[a].at[:, :, pl.ds(h * cw, cw)], list(range(1, bits)))
    pending = []
    for step in range(bits - 1):
        todo = []
        for a in range(na):
            for h in range(2):
                src, free = state[a, h]
                b = orders[h][step]
                at = free.index(b)
                lo = 1 << at
                left = [f for f in free if f != b]
                cnt = 1 << len(left)
                recv, out = half_refs[pos], half_refs[pos + 1]
                sem_s, sem_r = half_refs[pos + 2], half_refs[pos + 3]
                pos += 4
                items = []
                for i in range(cnt):
                    base = (i // lo) * 2 * lo + i % lo
                    keep = base + lo * mine[b]
                    give = base + lo * (1 - mine[b])
                    c = functools.partial(
                        remote, src.at[give], recv.at[i], sem_s.at[i], sem_r.at[i], partner[b]
                    )
                    c().start()
                    items.append((c, keep, i))
                todo.append((a, h, src, recv, out, items))
                state[a, h] = (out, left)
        for a, h, src, recv, out, items in todo:
            cw = ins[a].shape[2] // 2
            for c, keep, i in items:
                c().wait_recv()
                if step == bits - 2:
                    outs[a][:, pl.ds(h * cw, cw)] = src[keep] + recv[i]
                else:
                    out[i] = src[keep] + recv[i]
                pending.append(c)
    for c in pending:
        c().wait_send()
    for a in range(na):
        for i in range(ndp // 2):
            first(a, i).wait_send()
    for k in range(1, nz):
        gzc(k, z).wait_send()
    for j in range(1, ndp):
        sml(j, dp).wait_send()
        prt(j, dp).wait_send()
        row = lax.rem(dp + ndp - j, ndp)
        sml(j, row).wait_recv()
        prt(j, row).wait_recv()
    for c in own:
        c().wait()


def reduce_over_dp(arrays, small, part, ndp, nz, cid):
    na = len(arrays)
    bits = ndp.bit_length() - 1
    sd = jax.ShapeDtypeStruct
    dma = pltpu.SemaphoreType.DMA
    scratch = [pltpu.VMEM((ndp // 2,) + a.shape[1:], F32) for a in arrays] * 2
    for step in range(bits - 1):
        cnt = ndp >> (step + 2)
        for a in arrays:
            for h in range(2):
                shape = (cnt, a.shape[1], a.shape[2] // 2)
                scratch += [pltpu.VMEM(shape, F32), pltpu.VMEM(shape, F32), dma((cnt,)), dma((cnt,))]
    scratch += [
        pltpu.VMEM((nz,) + part.shape, F32),
        dma((na, ndp // 2)),
        dma((na, ndp // 2)),
        dma((2, ndp - 1)),
        dma((2, ndp - 1)),
        dma((nz - 1,)),
        dma((nz - 1,)),
        dma((2,)),
    ]
    return pl.pallas_call(
        functools.partial(reduce_kernel, ndp, nz, na),
        out_shape=[sd(a.shape[1:], F32) for a in arrays]
        + [sd((ndp,) + small.shape, F32), sd((ndp, nz) + part.shape, F32)],
        in_specs=[VMEM] * (na + 2),
        out_specs=[VMEM] * (na + 2),
        scratch_shapes=scratch,
        compiler_params=pltpu.CompilerParams(
            collective_id=cid, has_side_effects=True, vmem_limit_bytes=56 << 20
        ),
    )(*arrays, small, part)


def swap_halves(u):
    n = u.shape[1]
    lane = lax.broadcasted_iota(jnp.int32, u.shape, 1)
    half = HEAD_DIM // 2
    return jnp.where(
        lane % HEAD_DIM < half, pltpu.roll(u, n - half, 1), pltpu.roll(u, half, 1)
    )


QB = 256
KB = 256
NEG = -1e30


def stack_heads(dst, src, heads):
    lane = lax.broadcasted_iota(jnp.int32, src.shape, 1) // HEAD_DIM
    for h in range(heads):
        dst[:, h] = jnp.where(lane == h, src, jnp.zeros_like(src)).reshape(dst.shape[0], dst.shape[2], dst.shape[3])

def fwd_kernel(heads, QB, KB, lo_ref, hi_ref, q_ref, k_ref, v_ref, segq_ref, segk_ref, o_ref, lse_ref, vt_ref, ks_ref, s_ref):
    i = pl.program_id(1)
    @pl.when(i == 0)
    def _():
        vt_ref[...] = v_ref[...].T
        stack_heads(ks_ref, k_ref[...], heads)
    q = q_ref[...]
    segq = segq_ref[0, pl.ds(0, 1)]
    e = q.shape[1]
    lo, hi = lo_ref[i], hi_ref[i]
    def first(j, mx):
        start = pl.multiple_of(j*KB, KB)
        s = dot(ks_ref[j].reshape(heads*KB, e), q, NT)
        segk = segk_ref[pl.ds(start, KB), :]
        same = jnp.concatenate([segk]*(QB//128), axis=1) == segq
        out = []
        for h in range(heads):
            sh = jnp.where(same, s[h*KB:(h+1)*KB], NEG)
            s_ref[j, h] = sh
            out.append(jnp.maximum(mx[h], jnp.max(sh.reshape(KB//8, 8, QB), axis=0)))
        return out
    mx = lax.fori_loop(lo, hi, first, [jnp.full((8, QB), NEG, F32)]*heads)
    ms = [jnp.max(m, axis=0, keepdims=True) for m in mx]
    def second(j, carry):
        ls, os_ = carry
        start = pl.multiple_of(j*KB, KB)
        nl, no = [], []
        for h in range(heads):
            p = jnp.exp(s_ref[j, h] - ms[h])
            nl.append(ls[h] + jnp.sum(p.reshape(KB//8, 8, QB), axis=0))
            vt = vt_ref[pl.ds(h*HEAD_DIM, HEAD_DIM), pl.ds(start, KB)]
            no.append(os_[h] + dot(vt, p.astype(BF16)))
        return nl, no
    ls, os_ = lax.fori_loop(lo, hi, second, ([jnp.zeros((8, QB), F32)]*heads, [jnp.zeros((HEAD_DIM, QB), F32)]*heads))
    l1 = [jnp.sum(l, axis=0, keepdims=True) for l in ls]
    out = jnp.concatenate([os_[h] / l1[h] for h in range(heads)], axis=0)
    o_ref[...] = out.T.astype(BF16)
    lse = [ms[h] + jnp.log(l1[h]) for h in range(heads)]
    lse_ref[0] = jnp.concatenate(lse + [jnp.zeros((8 - heads, QB), F32)], axis=0)

def attn_fwd(q, k, v, seg_row, seg_col, lo, hi, groups, QB=QB, KB=KB):
    t = q.shape[0]; e = q.shape[1]//groups; heads = e//HEAD_DIM
    return pl.pallas_call(functools.partial(fwd_kernel, heads, QB, KB),
        out_shape=[jax.ShapeDtypeStruct(q.shape, BF16), jax.ShapeDtypeStruct((groups, 8, t), F32)],
        grid_spec=pltpu.PrefetchScalarGridSpec(num_scalar_prefetch=2, grid=(groups, t//QB),
            in_specs=[pl.BlockSpec((QB, e), lambda g,i,*_: (i, g)), pl.BlockSpec((t, e), lambda g,i,*_: (0, g)), pl.BlockSpec((t, e), lambda g,i,*_: (0, g)),
                      pl.BlockSpec((1, 8, QB), lambda g,i,*_: (0,0,i)), pl.BlockSpec((t,128), lambda g,i,*_: (0,0))],
            out_specs=[pl.BlockSpec((QB, e), lambda g,i,*_: (i, g)), pl.BlockSpec((1,8,QB), lambda g,i,*_: (g,0,i))],
            scratch_shapes=[pltpu.VMEM((e,t),BF16), pltpu.VMEM((t//KB, heads, KB, e), BF16), pltpu.VMEM((t//KB, heads, KB, QB), F32)]),
        compiler_params=pltpu.CompilerParams(vmem_limit_bytes=56<<20))(lo, hi, q, k, v, seg_row, seg_col)

def bwd_kernel(heads, QB, KB, lo_ref, hi_ref, q_ref, k_ref, v_ref, att_ref, g_ref, lse_ref, segq_ref, segk_ref, cos_ref, sin_ref, gq_ref, gk_ref, gv_ref,
               kt_ref, ks_ref, vs_ref, dk_ref, dv_ref):
    t, e = k_ref.shape
    kt_ref[...] = k_ref[...].T
    stack_heads(ks_ref, k_ref[...], heads)
    stack_heads(vs_ref, v_ref[...], heads)
    dk_ref[...] = jnp.zeros_like(dk_ref); dv_ref[...] = jnp.zeros_like(dv_ref)
    row = lax.broadcasted_iota(jnp.int32, (8, e), 0); lane = lax.broadcasted_iota(jnp.int32, (8, e), 1)
    ind = jnp.where(lane//HEAD_DIM == row, 1.0, 0.0).astype(F32)
    lanek = lax.broadcasted_iota(jnp.int32, (KB, e), 1)//HEAD_DIM
    @pl.loop(0, t//QB)
    def _(i):
        qs = pl.multiple_of(i*QB, QB)
        q = q_ref[pl.ds(qs, QB), :]; g = g_ref[pl.ds(qs, QB), :]
        segq = segq_ref[0, pl.ds(0,1), pl.ds(qs, QB)]
        prod = g.astype(F32)*att_ref[pl.ds(qs, QB), :].astype(F32)
        delta = dot(ind, prod, NT, lax.Precision.HIGHEST)
        lse = lse_ref[0, :, pl.ds(qs, QB)]
        def body(j, dq):
            start = pl.multiple_of(j*KB, KB)
            s = dot(ks_ref[j].reshape(heads*KB, e), q, NT)
            dpt = dot(vs_ref[j].reshape(heads*KB, e), g, NT)
            segk = segk_ref[pl.ds(start, KB), :]
            same = jnp.concatenate([segk]*(QB//128), axis=1) == segq
            ps, dss, ndq = [], [], []
            for h in range(heads):
                p = jnp.exp(jnp.where(same, s[h*KB:(h+1)*KB], NEG) - lse[h:h+1])
                ds = (p*(dpt[h*KB:(h+1)*KB] - delta[h:h+1])).astype(BF16)
                ps.append(p.astype(BF16)); dss.append(ds)
                kt = kt_ref[pl.ds(h*HEAD_DIM, HEAD_DIM), pl.ds(start, KB)]
                ndq.append(dq[h] + dot(kt, ds))
            dvs = dot(jnp.concatenate(ps, axis=0), g)
            dks = dot(jnp.concatenate(dss, axis=0), q)
            dv, dk = dvs[:KB], dks[:KB]
            for h in range(1, heads):
                dv = jnp.where(lanek == h, dvs[h*KB:(h+1)*KB], dv)
                dk = jnp.where(lanek == h, dks[h*KB:(h+1)*KB], dk)
            dk_ref[pl.ds(start, KB), :] += dk
            dv_ref[pl.ds(start, KB), :] += dv
            return ndq
        dq = lax.fori_loop(lo_ref[i], hi_ref[i], body, [jnp.zeros((HEAD_DIM, QB), F32)]*heads)
        dqf = jnp.concatenate(dq, axis=0).T * (HEAD_DIM**-0.5)
        cos = cos_ref[pl.ds(qs, QB), :]; sin = sin_ref[pl.ds(qs, QB), :]
        gq_ref[pl.ds(qs, QB), :] = (dqf*cos - swap_halves(dqf)*sin).astype(BF16)
    dk = dk_ref[...]
    gk_ref[...] = (dk*cos_ref[...] - swap_halves(dk)*sin_ref[...]).astype(BF16)
    gv_ref[...] = dv_ref[...].astype(BF16)

def attn_bwd(q,k,v,att,g,lse,seg_row,seg_col,lo,hi,cos,sin,groups,QB=QB,KB=KB):
    t = q.shape[0]; e = q.shape[1]//groups; heads = e//HEAD_DIM
    col = pl.BlockSpec((t,e), lambda g,*_: (0,g)); full = lambda s: pl.BlockSpec(s, lambda g,*_: (0,0))
    return pl.pallas_call(functools.partial(bwd_kernel, heads, QB, KB), out_shape=[jax.ShapeDtypeStruct(q.shape,BF16)]*3,
        grid_spec=pltpu.PrefetchScalarGridSpec(num_scalar_prefetch=2, grid=(groups,),
            in_specs=[col]*5+[pl.BlockSpec((1,8,t), lambda g,*_: (g,0,0)), pl.BlockSpec((1,8,t), lambda g,*_: (0,0,0)), full((t,128)), full((t,e)), full((t,e))],
            out_specs=[col]*3,
            scratch_shapes=[pltpu.VMEM((e,t),BF16), pltpu.VMEM((t//KB,heads,KB,e),BF16), pltpu.VMEM((t//KB,heads,KB,e),BF16), pltpu.VMEM((t,e),F32), pltpu.VMEM((t,e),F32)]),
        compiler_params=pltpu.CompilerParams(vmem_limit_bytes=58<<20))(lo,hi,q,k,v,att,g,lse,seg_row,seg_col,cos,sin)


def gnormed_kernel(gq_ref, gk_ref, gv_ref, wq_ref, wk_ref, wv_ref, w_ref, o_ref):
    g = pl.program_id(0)
    grads = (gq_ref, gk_ref, gv_ref)
    own = (wq_ref, wk_ref, wv_ref)

    @pl.when(g == 0)
    def _():
        o_ref[...] = dot(gq_ref[...], wq_ref[...], NT)
        for a in (1, 2):
            o_ref[...] += dot(grads[a][...], own[a][...], NT)

    @pl.when(g > 0)
    def _():
        for a in range(3):
            o_ref[...] += dot(grads[a][...], w_ref[0, a].astype(BF16), NT)


def gnormed(gq, gk, gv, wq, wk, wv, w):
    t = gq.shape[0]
    d, e = wq.shape
    groups = w.shape[0] + 1
    full = lambda s: pl.BlockSpec(s, lambda g: (0, 0))
    return pl.pallas_call(
        gnormed_kernel,
        grid=(groups,),
        out_shape=jax.ShapeDtypeStruct((t, d), F32),
        in_specs=[pl.BlockSpec((t, e), lambda g: (0, g))] * 3
        + [full((d, e))] * 3
        + [pl.BlockSpec((1, 3, d, e), lambda g: (jnp.maximum(g - 1, 0), 0, 0, 0))],
        out_specs=full((t, d)),
        compiler_params=pltpu.CompilerParams(vmem_limit_bytes=56 << 20),
    )(gq, gk, gv, wq, wk, wv, w)


def stats(values):
    mean_val = jnp.mean(values, axis=-1, keepdims=True)
    centred = values - mean_val
    r = lax.rsqrt(jnp.mean(centred * centred, axis=-1, keepdims=True) + EPS)
    return centred * r, r


def norm_pull(x, r, scale, grad):
    gp = grad * (1.0 + scale)
    return r * (
        gp - jnp.mean(gp, axis=-1, keepdims=True) - x * jnp.mean(gp * x, axis=-1, keepdims=True)
    )


def time_freqs(width):
    half = width // 2
    return jnp.exp(-math.log(10000.0) * jnp.arange(half, dtype=F32) / half)


def time_embed(flow_time, width):
    angles = 1000.0 * flow_time[:, None] * time_freqs(width)[None, :]
    both = jnp.concatenate([jnp.cos(angles), jnp.sin(angles)], axis=1)
    return jax.nn.silu(both).astype(BF16)


def per_device(ndp, nz, *args):
    (
        frames,
        skip_in,
        flow_time,
        segment_ids,
        w_skip,
        b_skip,
        w_mod,
        b_mod,
        w_q,
        w_k,
        w_v,
        w_o,
        w_up,
        b_up,
        w_dn,
        b_dn,
        out_grad,
    ) = args
    t, d = frames.shape
    loc = w_q.shape[1]
    fl = w_up.shape[1]
    dp = lax.axis_index("dp")
    z = lax.axis_index("tensor")
    embed = time_embed(flow_time, d)
    mod_part = dot(embed, w_mod)[0] + b_mod
    own_small = jnp.concatenate([mod_part, b_skip, b_up])[None, :]

    seg = segment_ids[0]
    idx = jnp.arange(t, dtype=jnp.int32)
    nseg = 4
    starts = jnp.stack([jnp.sum((seg < s).astype(jnp.int32)) for s in range(nseg + 1)])
    first_at = jnp.zeros_like(seg)
    for s in range(1, nseg):
        first_at = jnp.where(seg >= s, starts[s], first_at)
    pos = (idx - first_at).astype(F32)
    half = HEAD_DIM // 2
    inv = jnp.exp(-math.log(10000.0) * 2.0 * jnp.arange(half, dtype=F32) / HEAD_DIM)
    ang = pos[:, None] * inv[None, :]
    cos_h, sin_h = jnp.cos(ang), jnp.sin(ang)
    cos = jnp.tile(cos_h, (1, loc // half))
    sin = jnp.tile(jnp.concatenate([-sin_h, sin_h], axis=1), (1, loc // HEAD_DIM))
    qb_first, qb_last = seg[::QB], seg[QB - 1 :: QB]
    lo = jnp.take(starts, qb_first) // KB
    hi = (jnp.take(starts, qb_last + 1) + KB - 1) // KB
    seg_row = jnp.broadcast_to(seg[None, None, :], (1, 8, t))
    seg_col = jnp.broadcast_to(seg[:, None], (t, 128))

    hidden, normed, q, k, v, wskip, wqkv, wo, small = first(
        frames, skip_in, w_skip, w_q, w_k, w_v, w_o, own_small, cos, sin, nz
    )
    small = small[:, 0]
    nm = mod_part.shape[0]
    mod = small[:, :nm].reshape(6, d)
    shift1, scale1, gate1, shift2, scale2, gate2 = [mod[i][None, :] for i in range(6)]
    bup = jnp.concatenate(
        [
            lax.dynamic_index_in_dim(small[:, nm + loc :], (z + k) % nz, 0, keepdims=True)
            for k in range(1, nz)
        ]
    )

    def own_cols(a):
        return lax.dynamic_slice_in_dim(a, z * loc, loc, a.ndim - 1)

    att, lse = attn_fwd(q, k, v, seg_row, seg_col, lo, hi, nz)
    output, g_mid, g_branch, g_att, gw, sums, g_b_up, g_gate2_own, _ = second(
        att,
        hidden,
        out_grad,
        w_o,
        wo,
        w_up,
        w_dn,
        jnp.concatenate([mod, jnp.zeros((2, d), F32)]),
        b_up[None, :],
        bup,
        b_dn[None, :],
        nz,
    )
    g_shift2, g_scale2, g_gate1 = sums[0], sums[1], sums[2]
    g_b_dn = gate2[0] * sums[3]
    first_sum = lax.psum_scatter(gw, "dp", scatter_dimension=1, tiled=True)
    gq, gk, gv = attn_bwd(q, k, v, att, g_att, lse, seg_row, seg_col, lo, hi, cos, sin, nz)
    x1, r1 = stats(hidden)
    g_normed = gnormed(gq, gk, gv, w_q, w_k, w_v, wqkv)
    g_qkv = jnp.concatenate([gq[:, :loc], gk[:, :loc], gv[:, :loc]], axis=1)
    g_w_qkv = dot(normed, g_qkv, TN)
    g_shift1 = jnp.sum(g_normed, axis=0)
    g_scale1 = jnp.sum(g_normed * x1, axis=0)
    g_hidden = g_mid + norm_pull(x1, r1, scale1, g_normed)
    g_low = g_hidden.astype(BF16)
    own_low = own_cols(g_low)
    g_b_skip = jnp.sum(own_cols(g_hidden), axis=0)
    g_w_skip = jnp.concatenate([dot(frames, own_low, TN), dot(skip_in, own_low, TN)], axis=0)

    def rows_of(base):
        return lax.dynamic_slice_in_dim(wskip, base + z * loc, loc, 0).astype(BF16)

    grad_frames = dot(g_low, rows_of(0), NT)
    grad_skip = dot(g_low, rows_of(d), NT)

    g_mod = jnp.concatenate(
        [g_shift1, g_scale1, g_gate1, g_shift2, g_scale2, jnp.zeros((d,), F32)]
    )
    own_mod = lax.dynamic_slice_in_dim(g_mod, z * nm, nm, 0)
    sizes = [nm, loc, fl, d, 128]
    offs = [sum(sizes[:i]) for i in range(len(sizes) + 1)]
    vec = jnp.concatenate(
        [own_mod, g_b_skip, g_b_up[0], g_b_dn, jnp.broadcast_to(flow_time, (128,))]
    )[None, :]
    s_qkv, s_w_skip, vecs, gates = reduce_over_dp(
        [g_w_qkv.reshape(ndp, d // ndp, 3 * loc), g_w_skip.reshape(ndp, 2 * d // ndp, loc)],
        vec,
        g_gate2_own,
        ndp,
        nz,
        1,
    )
    vecs = vecs[:, 0]
    gate_all = gates.reshape(ndp, d)
    pad = jnp.concatenate([jnp.zeros((ndp, 5 * d), F32), gate_all], axis=1)
    mod_rows = vecs[:, :nm] + lax.dynamic_slice_in_dim(pad, z * nm, nm, 1)

    def share(i, of):
        n = sizes[i] // ndp
        cols = lax.dynamic_slice_in_dim(of, offs[i] + dp * n, n, 1)
        return jnp.sum(cols, axis=0)

    def mine(v):
        n = v.shape[1] // ndp
        return jnp.sum(lax.dynamic_slice_in_dim(v, dp * n, n, 1), axis=0)

    s_b_mod = mine(mod_rows)
    embeds = time_embed(vecs[:, offs[4]], d)
    rows = d // ndp
    s_w_mod = dot(lax.dynamic_slice_in_dim(embeds, dp * rows, rows, 1), mod_rows.astype(BF16), TN)
    s_up = first_sum[:fl].T
    s_dn = first_sum[fl : 2 * fl]
    s_o = first_sum[2 * fl :]
    return (
        output,
        grad_frames,
        grad_skip,
        s_w_skip,
        share(1, vecs),
        s_w_mod,
        s_b_mod,
        s_qkv[:, :loc],
        s_qkv[:, loc : 2 * loc],
        s_qkv[:, 2 * loc :],
        s_o,
        s_up,
        share(2, vecs),
        s_dn,
        share(3, vecs),
    )


def solution(mesh):
    in_specs = (
        P("dp", None),
        P("dp", None),
        P("dp"),
        P("dp", None),
        P(None, "tensor"),
        P("tensor"),
        P(None, "tensor"),
        P("tensor"),
        P(None, "tensor"),
        P(None, "tensor"),
        P(None, "tensor"),
        P("tensor", None),
        P(None, "tensor"),
        P("tensor"),
        P("tensor", None),
        P(),
        P("dp", None),
    )
    out_specs = (
        P("dp", "tensor"),
        P("dp", "tensor"),
        P("dp", "tensor"),
        P("dp", "tensor"),
        P(("tensor", "dp")),
        P("dp", "tensor"),
        P(("tensor", "dp")),
        P("dp", "tensor"),
        P("dp", "tensor"),
        P("dp", "tensor"),
        P("tensor", "dp"),
        P("dp", "tensor"),
        P(("tensor", "dp")),
        P("tensor", "dp"),
        P("dp"),
    )
    return jax.shard_map(
        functools.partial(per_device, mesh.shape["dp"], mesh.shape["tensor"]),
        mesh=mesh,
        in_specs=in_specs,
        out_specs=out_specs,
        check_vma=False,
    )
```

time: 782 us -> 598 us (0.76)
  matrix products: 135 us -> 16.2 us
  other arithmetic: 78.1 us -> 21.5 us
  local copies, waits for them, and re-layouts: 59.9 us -> 31.3 us
  Pallas kernels: 490 us -> 510 us
    dot_general x33 -> x7, matrix products: 135 us -> 16.2 us  [dot(): lax.dot_general(a, b, dims, precision=precision, preferred_element_type=F32)]
    another operation x5 -> x0, other arithmetic: 25 us -> none
    pallas_call x4, Pallas kernels: 441 us -> 461 us  [the longest x1 201 us: second(): pl.pallas_call(functools.partial(second_kernel, nz, n, r, per), out_shape...]
    convert_element_type x9 -> x1, other arithmetic: 18.2 us -> 2.63 us  [per_device(): pos = (idx - first_at).astype(F32)]
    unnamed x121 -> x45, local copies, waits for them, and re-layouts: 19.1 us -> 6.33 us
    another operation x2, local copies, waits for them, and re-layouts: 13.7 us -> 1.42 us  [per_device(): jnp.tile(jnp.concatenate([-sin_h, sin_h], axis=1), (1, loc // HEAD_DIM))]
    concatenate x3 -> x2, other arithmetic: 10.8 us -> 0.16 us  [the longest x1 0.14 us: per_device(): jnp.concatenate([dot(frames, own_low, TN), dot(skip_in, own_low, TN)], ax...]
  transfers between devices with their start and end apart: 1 -> 1, of which waited for: 0 -> 0; matrix products, arithmetic and copies ran while one was open for 8% -> 7% of each run, Pallas kernels for 21% -> 19%
where the time goes in v2:
time: 598 us; the launch traced here: 594 us
  Pallas kernels  510 us (85%)
  local copies, waits for them, and re-layouts  31.3 us (5%)
  other arithmetic  21.5 us (4%)
  matrix products  16.2 us (3%)
  between operations  15.4 us (3%)
    pallas_call x1, Pallas kernels, second(): pl.pallas_call(functools.partial(second_kernel, nz, n, r, per), out_shape...  201 us
    pallas_call x1, Pallas kernels, first(): pl.pallas_call(functools.partial(first_kernel, nz, chunks), out_shape=out...  154 us
    pallas_call x1, Pallas kernels, attn_bwd(): pl.pallas_call(functools.partial(bwd_kernel, heads, QB, KB), out_shape=[j...  66.9 us
    pallas_call x1, Pallas kernels, attn_fwd(): pl.pallas_call(functools.partial(fwd_kernel, heads, QB, KB), out_shape=[j...  39 us
    pallas_call x1, Pallas kernels, reduce_over_dp(): pl.pallas_call(functools.partial(reduce_kernel, ndp, nz, na), out_shape=[...  35.8 us
    dot_general x7, matrix products, dot(): lax.dot_general(a, b, dims, precision=precision, preferred_element_type=F32)  16.2 us
    pallas_call x1, Pallas kernels, gnormed(): pl.pallas_call(gnormed_kernel, grid=(groups,), out_shape=jax.ShapeDtypeSt...  13.1 us
  transfers between devices with their start and end apart: 1, of which 0 were waited for; matrix products, arithmetic and copies ran while one was open for 7% of the time, Pallas kernels for 19%

profile of v2, /device:TPU:0, one launch (start us, length us, event | category | flops | bytes accessed | tf_op | source)
XLA Modules:
  0.0 594.1 jit_solution(6974209970727872702)
XLA Ops:
  7.2 0.0 reduce-scatter.2.cloned.1.call-start
  7.3 1.4 convert_reduce_fusion
  8.7 0.8 slice.65
  9.4 0.8 slice.66
  10.2 2.6 subtract_convert_fusion
  12.9 0.5 fusion.11
  13.4 0.1 tile.20
  13.5 1.3 copy.36.refs_9_.sin_ref
  14.9 0.1 tile.8
  15.0 1.3 copy.35.refs_8_.cos_ref
  17.0 2.4 convolution_reduce_fusion
  19.5 0.6 broadcast_in_dim.56.refs_7_
  20.1 154.2 %shard_map.280 = (f32[1024,1024]{1,0:T(8,128)}, bf16[1024,1024]{1,0:T(8,128)(2,1)}, bf16[1024,1024]{1,0:T(8,128)(2,1)}, bf16[1024,1024]{1,0:T(8,128)(2,1)}, bf16...) custom-call(bf16[1024,1024]{1,0:T(8,128)(2,1)} %refs_0_.1, ...), custom_call_target="tpu_custom_call" | custom-call | tf_op jit(solution)/shard_map/pallas_call | solution.py:314
  174.3 0.8 copy.50
  175.2 0.3 reshape.182
  175.5 0.1 copy.48
  175.6 0.7 reshape.183.refs_9_
  176.3 3.3 stack.23
  179.7 0.6 gather_fusion.1
  180.3 0.5 and_select_fusion.2.hi_ref
  180.8 0.6 gather_fusion
  181.5 0.5 and_select_fusion.3.lo_ref
  182.0 0.6 concatenate.42.refs_7_
  182.6 1.0 broadcast_in_dim.61.segk_ref
  183.6 0.6 broadcast_in_dim.60.segq_ref
  184.3 39.0 %shard_map.281 = (bf16[1024,1024]{1,0:T(8,128)(2,1)}, f32[4,8,1024]{2,1,0:T(8,128)}) custom-call(s32[4]{0:T(128)} %and_select_fusion.3.lo_ref, s32[4]{0:T(128)} %and_select_fusion.2.hi_ref, bf16[1024,1024]{1,0:T(8,128)(2,1)} %get-tuple-element.41.q_ref, bf16[1024,1024]{1,0:T(8,128)(2,1)} %get-tuple-element.42.k_ref, ...), custom_call_target="tpu_custom_call" | custom-call | tf_op jit(solution)/shard_map/pallas_call | solution.py:768
  223.2 200.7 %shard_map.282 = (f32[1024,256]{1,0:T(8,128)}, f32[1024,1024]{1,0:T(8,128)}, bf16[1024,1024]{1,0:T(8,128)(2,1)}, bf16[1024,1024]{1,0:T(8,128)(2,1)}, f32[2304,10...) custom-call(bf16[1024,1024]{1,0:T(8,128)(2,1)} %get-tuple-element.44, ...), custom_call_target="tpu_custom_call" | custom-call | tf_op jit(solution)/shard_map/pallas_call | solution.py:539
  424.0 2.5 reduce_sum.149
  426.4 66.9 %shard_map.283 = (bf16[1024,1024]{1,0:T(8,128)(2,1)}, bf16[1024,1024]{1,0:T(8,128)(2,1)}, bf16[1024,1024]{1,0:T(8,128)(2,1)}) custom-call(s32[4]{0:T(128)} %and_select_fusion.3.lo_ref, s32[4]{0:T(128)} %and_select_fusion.2.hi_ref, bf16[1024,1024]{1,0:T(8,128)(2,1)} %get-tuple-element.41.q_ref, bf16[1024,1024]{1,0:T(8,128)(2,1)} %get-tuple-element.42.k_ref, ...), custom_call_target="tpu_custom_call" | custom-call | tf_op jit(solution)/shard_map/pallas_call | solution.py:828
  493.3 1.1 slice.70
  494.4 1.1 slice.71
  495.5 1.9 slice.72
  497.3 13.1 %shard_map.284 = f32[1024,1024]{1,0:T(8,128)} custom-call(bf16[1024,1024]{1,0:T(8,128)(2,1)} %get-tuple-element.52.gq_ref, bf16[1024,1024]{1,0:T(8,128)(2,1)} %get-tuple-element.53.gk_ref, bf16[1024,1024]{1,0:T(8,128)(2,1)} %get-tuple-element.54.gv_ref, bf16[1024,256]{1,0:T(8,128)(2,1)} %wq_ref.1, bf16[1024,256]{1,0:T(8,128)(2,1)} %wk_ref.1, ...), custom_call_target="tpu_custom_call" | custom-call | tf_op jit(solution)/shard_map/pallas_call | solution.py:858
  510.4 2.9 multiply_reduce_fusion.2
  513.4 0.5 copy-done
  513.9 4.0 multiply_reduce_fusion
  518.0 0.6 copy-done.6
  518.6 1.7 fusion.24
  520.4 0.2 dynamic-slice_reduce_fusion
  520.6 0.1 dynamic-slice_dynamic-update-slice_fusion
  520.7 0.6 broadcast_in_dim.67.refs_2_
  521.3 0.8 convolution_bitcast_fusion
  522.1 0.6 copy-done.3
  522.7 0.7 convolution_bitcast_fusion.1
  523.5 0.1 pad_maximum_fusion
  523.6 1.8 copy.40
  525.4 5.3 fusion
  530.7 35.8 %shard_map.285 = (f32[128,768]{1,0:T(8,128)}, f32[256,256]{1,0:T(8,128)}, f32[8,1,3968]{2,1,0:T(1,128)}, f32[8,4,1,256]{3,2,1,0:T(1,128)}) custom-call(f32[8,128,768]{2,1,0:T(8,128)} %bitcast.50, f32[8,256,256]{2,1,0:T(8,128)} %bitcast.47, f32[1,3968]{1,0:T(1,128)} %broadcast_in_dim.67.refs_2_, f32[1,256]{1,0:T(1,128)} %get-tuple-element.60.refs_3_), custom_call_target="tpu_custom_call" | custom-call | tf_op jit(solution)/shard_map/pallas_call | solution.py:694
  566.5 0.9 copy.49
  567.4 0.8 reduce.5
  568.3 0.7 dynamic-slice_reduce_fusion.1
  569.0 1.3 dynamic-slice_reduce_fusion.4
  570.3 1.2 dynamic-slice_reduce_fusion.2
  571.5 0.1 fusion.15
  571.6 0.1 multiply_cosine_fusion.1
  571.8 1.8 fusion.26
  573.5 1.2 fusion.12
  574.7 2.9 fusion.7
  577.7 2.9 fusion.6
  580.6 2.2 fusion.25
  582.8 1.0 copy.41
  583.8 1.6 slice.96
  585.4 1.0 copy.64
  586.3 0.7 copy.65
  (63 shorter events, 0.4 us)
Async XLA Ops:
  7.2 573.5 %reduce-scatter.2.cloned.1.call-start = ((), (), s32[]{:S(2)}) async-start(), calls=%async_computation.1 | async-start | bytes 10616832 | tf_op jit(solution)/shard_map/reduce_scatter | solution.py:978
  14.8 4.6 copy-start.11
  14.9 4.6 copy-start.10
  14.9 4.6 copy-start.14
  20.1 162.5 %copy-start.9 = (s32[1,1024]{1,0:T(1,128)S(1)}, s32[1,1024]{1,0:T(1,128)}, u32[]{:S(2)}) copy-start(s32[1,1024]{1,0:T(1,128)} %param.22) | copy-start | bytes 12292
  510.4 2.9 copy-start.12
  510.4 3.5 copy-start
  513.9 4.1 copy-start.1
  513.9 4.7 copy-start.6
  518.6 2.1 copy-start.13
  518.6 2.7 copy-start.2
  520.4 3.1 copy-start.4
  520.4 2.4 copy-start.3
  530.7 44.0 %copy-start.5 = (bf16[1024,1024]{1,0:T(8,128)(2,1)S(1)}, bf16[1024,1024]{1,0:T(8,128)(2,1)}, u32[]{:S(2)}) copy-start(bf16[1024,1024]{1,0:T(8,128)(2,1)} %copy-done.4) | copy-start | bytes 6291460
  580.6 4.7 copy-start.7
  580.6 5.7 copy-start.8
Sparse Core Ops, SparseCore 0:
  424.1 74.3 reduce-scatter.1
